TPU v7x, 32 devices: a whole 2x2x4 slice. The times are simulated.
32 devices in a mesh: slide: 4 (over x, core), rows: 8 (over z, y).
Axes of the slice: x: 2, y: 2, z: 4, core: 2. Of those that a mesh axis runs over, the one named last changes fastest.
Arguments:
- features: bfloat16 [4, 192, 256, 128], P('slide', None, 'rows'), may hold values from -6 to 6
- depth_kernel: float32 [192, 49], replicated, may hold values from -0.875 to 0.875
- depth_bias: float32 [192], replicated, may hold values from -4 to 4
- norm_gain: float32 [192], replicated, may hold values from 0.1 to 1.9
- norm_bias: float32 [192], replicated, may hold values from -3 to 3
- up_weight: bfloat16 [192, 768], replicated, may hold values from -0.4375 to 0.4375
- up_bias: float32 [768], replicated, may hold values from -3 to 3
- down_weight: bfloat16 [768, 192], replicated, may hold values from -0.21875 to 0.21875
- down_bias: float32 [192], replicated, may hold values from -4 to 4
- layer_scale: float32 [192], replicated, may hold values from 0.2 to 1
- tissue: int32 [4, 8, 4], P('slide', 'rows'), may hold values 0 or 1
- aggregator_order: int32 [4, 32], P('slide'), may hold values from 0 to 31, each once within a row
- tile_cotangent: bfloat16 [4, 32, 192], P('slide', 'rows'), may hold values from -6 to 6
Outputs:
- embedding: float32 [4, 32, 192], P('slide', 'rows')
- input_grad: bfloat16 [4, 192, 256, 128], P('slide', None, 'rows')
- grad_up: float32 [192, 768], replicated
- grad_down: float32 [768, 192], replicated
- grad_kernel: float32 [192, 49], replicated
Inputs may be any that keep to these rules, and one draw needn't show every extreme that they name: `aggregator_order`: each slide's row is a permutation of the 32 positions.
All inputs are finite; a program needn't handle non-finite values. No bound on the sum of `tissue` on one device may be relied on, other than what follows from the above.
Results may differ from a plain program's by a relative error of at most 0.0064.
Values may be sent and summed in bfloat16 or wider, within the bound.
A program may use at most 128 MiB of HBM per device.

v0:
```python
import math

import jax
import jax.numpy as jnp
from jax import lax
from jax.sharding import PartitionSpec as P

TILE = 32


def extended_2(cells, sides, width):
    for axis, dim in sides:
        count = lax.axis_size(axis)
        ends = count - 1
        head = lax.slice_in_dim(cells, 0, width, axis=dim)
        tail = lax.slice_in_dim(cells, cells.shape[dim] - width, cells.shape[dim], axis=dim)
        cells = jnp.concatenate(
            [
                lax.ppermute(tail, axis, [(i, (i + 1) % count) for i in range(ends)]),
                cells,
                lax.ppermute(head, axis, [((i + 1) % count, i) for i in range(ends)]),
            ],
            axis=dim,
        )
    return cells


def depthwise(source, kernel, height, across, mirrored):
    channels = source.shape[0]
    total = jnp.zeros((channels, height, across), jnp.float32)
    for position in range(49):
        row_start = position // 7
        col_start = position % 7
        if mirrored:
            row_start = 6 - row_start
            col_start = 6 - col_start
        window = lax.slice(
            source, (0, row_start, col_start), (channels, row_start + height, col_start + across)
        )
        total = total + kernel[:, position][:, None, None] * window.astype(jnp.float32)
    return total


def gelu_exact(values):
    return 0.5 * values * (1.0 + jax.scipy.special.erf(values * 0.7071067811865476))


def gelu_slope(values):
    cumulative = 0.5 * (1.0 + jax.scipy.special.erf(values * 0.7071067811865476))
    density = jnp.exp(-0.5 * values * values) * 0.3989422804014327
    return cumulative + values * density


def contract_first(left, right):
    return lax.dot_general(
        left, right, (((0,), (0,)), ((), ())), preferred_element_type=jnp.float32
    )


def contract_last(left, right):
    return lax.dot_general(
        left, right, (((1,), (1,)), ((), ())), preferred_element_type=jnp.float32
    )


def block_pass(
    conv_flat,
    image_flat,
    pixel_mask,
    pixel_cotangent,
    norm_gain,
    norm_bias,
    up_weight,
    up_bias,
    down_weight,
    down_bias,
    layer_scale,
):
    average = jnp.mean(conv_flat, axis=0, keepdims=True)
    centered = conv_flat - average
    variance = jnp.mean(centered * centered, axis=0, keepdims=True)
    reciprocal = lax.rsqrt(variance + 1e-06)
    standard = centered * reciprocal
    normed = (standard * norm_gain[:, None] + norm_bias[:, None]).astype(jnp.bfloat16)
    activation_in = contract_first(up_weight, normed) + up_bias[:, None]
    hidden = gelu_exact(activation_in).astype(jnp.bfloat16)
    branch = contract_first(down_weight, hidden) + down_bias[:, None]
    scaled_mask = pixel_mask[None, :] * layer_scale[:, None]
    output = image_flat.astype(jnp.float32) + scaled_mask * branch
    grad_branch = (scaled_mask * pixel_cotangent).astype(jnp.bfloat16)
    grad_hidden = jnp.dot(down_weight, grad_branch, preferred_element_type=jnp.float32)
    grad_activation = (grad_hidden * gelu_slope(activation_in)).astype(jnp.bfloat16)
    grad_normed = jnp.dot(up_weight, grad_activation, preferred_element_type=jnp.float32)
    grad_standard = grad_normed * norm_gain[:, None]
    grad_conv = reciprocal * (
        grad_standard
        - jnp.mean(grad_standard, axis=0, keepdims=True)
        - standard * jnp.mean(grad_standard * standard, axis=0, keepdims=True)
    )
    grad_conv = grad_conv.astype(jnp.bfloat16)
    up_term = contract_last(normed, grad_activation)
    down_term = contract_last(grad_branch, hidden)
    return (output, grad_conv, up_term, down_term)


def on_device(
    features,
    depth_kernel,
    depth_bias,
    norm_gain,
    norm_bias,
    up_weight,
    up_bias,
    down_weight,
    down_bias,
    layer_scale,
    tissue,
    aggregator_order,
    tile_cotangent,
):
    pixels_in = features[0]
    channels, height, across = pixels_in.shape
    tile_size = TILE
    tiles_here = across // tile_size
    hidden_units = up_weight.shape[1]
    extended = extended_2(pixels_in, (("rows", 1),), 3)
    extended = jnp.pad(extended, ((0, 0), (0, 0), (3, 3)))
    convolved = depthwise(extended, depth_kernel, height, across, False) + depth_bias[:, None, None]
    tile_masks = tissue[0, 0].astype(jnp.float32)
    pixel_mask = jnp.broadcast_to(
        tile_masks[None, :, None], (height, tiles_here, tile_size)
    ).reshape(height * across)
    gathered = lax.all_gather(tile_cotangent, "rows", axis=1, tiled=True)[0]
    positions = lax.dynamic_slice_in_dim(
        aggregator_order[0], lax.axis_index("rows") * tiles_here, tiles_here
    )
    wanted = jnp.take(gathered, positions, axis=0).astype(jnp.float32)
    pixel_cotangent = jnp.broadcast_to(
        wanted.T[:, None, :, None], (channels, height, tiles_here, tile_size)
    ).reshape(channels, height * across)
    output, grad_conv, up_term, down_term = block_pass(
        convolved.reshape(channels, height * across),
        pixels_in.reshape(channels, height * across),
        pixel_mask,
        pixel_cotangent,
        norm_gain,
        norm_bias,
        up_weight,
        up_bias,
        down_weight,
        down_bias,
        layer_scale,
    )
    embedding = jnp.mean(output.reshape(channels, height, tiles_here, tile_size), axis=(1, 3)).T[
        None
    ]
    grad_image = grad_conv.reshape(channels, height, across)
    grad_extended = extended_2(grad_image, (("rows", 1),), 3)
    grad_extended = jnp.pad(grad_extended, ((0, 0), (0, 0), (3, 3)))
    backward_conv = depthwise(grad_extended, depth_kernel, height, across, True)
    input_grad = (pixel_cotangent.reshape(channels, height, across) + backward_conv).astype(
        jnp.bfloat16
    )[None]
    kernel_cols = []
    for position in range(49):
        row_start = position // 7
        col_start = position % 7
        window = lax.slice(
            extended, (0, row_start, col_start), (channels, row_start + height, col_start + across)
        )
        kernel_cols.append(
            jnp.einsum("chw,chw->c", grad_image, window, preferred_element_type=jnp.float32)
        )
    kernel_term = jnp.stack(kernel_cols, axis=1)
    loss_norm = 1.0 / math.sqrt(lax.axis_size("slide") * lax.axis_size("rows") * height * across)
    combined = (
        jnp.concatenate(
            [up_term, down_term, kernel_term, jnp.zeros((channels, 15), jnp.float32)], axis=1
        )
        * loss_norm
    )
    totals = lax.psum(combined, ("slide", "rows"))
    grad_up = totals[:, :hidden_units]
    grad_down = totals[:, hidden_units : 2 * hidden_units].T
    grad_kernel = totals[:, 2 * hidden_units : 2 * hidden_units + 49]
    return (embedding, input_grad, grad_up, grad_down, grad_kernel)


def solution(mesh):
    return jax.shard_map(
        on_device,
        mesh=mesh,
        in_specs=(
            P("slide", None, "rows", None),
            P(),
            P(),
            P(),
            P(),
            P(),
            P(),
            P(),
            P(),
            P(),
            P("slide", "rows", None),
            P("slide", None),
            P("slide", "rows", None),
        ),
        out_specs=(P("slide", "rows", None), P("slide", None, "rows", None), P(), P(), P()),
        check_vma=False,
    )
```

profile of v0, /device:TPU:0, one launch (start us, length us, event | category | flops | bytes accessed | tf_op | source)
XLA Modules:
  0.0 483.2 jit_solution(3109074101789072919)
XLA Ops:
  8.6 4.9 %collective-permute-start = (bf16[192,3,128]{2,1,0:T(4,128)(2,1)S(1)}, bf16[192,3,128]{2,1,0:T(4,128)(2,1)S(1)}, u32[]{:S(2)}, u32[]{:S(2)}) collective-permute-start(bf16[192,3,128]{2,1,0:T(4,128)(2,1)S(1)} %get-tuple-element.81), channel_id=1, source_target_pairs={{0,1},{1,2},{2,3},{3,4},{4,5},{5,6},{6,7},{8,9},{9,10},{10,11},{11... | collective-permute-start | bytes 442376 | tf_op jit(solution)/shard_map/ppermute | solution.py:19
  16.0 1.6 fusion.164
  20.0 32.9 %all_gather.3 = bf16[1,32,192]{2,0,1:T(2,128)(2,1)S(1)} all-gather(bf16[1,4,192]{2,0,1:T(2,128)(2,1)S(1)} %copy.129), channel_id=1, replica_groups=mesh['slide'=4,'rows'=8] {'rows'}, dimensions={1}, use_global_device_ids=true | all-gather | bytes 13824 | tf_op jit(solution)/shard_map/all_gather | solution.py:133
  53.6 2.4 broadcast_in_dim.55
  56.0 5.4 %copy.131 = f32[192,4096]{1,0:T(8,128)} copy(f32[192,4096]{0,1:T(8,128)} %bitcast.261) | data formatting | bytes 6291456 | tf_op jit(solution)/shard_map/reshape | solution.py:140
  61.8 2.1 convert.150
  63.9 1.5 fusion.165
  65.5 4.7 select_maximum_fusion.2
  70.6 95.8 %fusion.159 = (f32[32,128]{1,0:T(8,128)S(1)}, f32[192,32,128]{2,1,0:T(8,128)}) fusion(f32[192]{0:T(256)S(1)} %copy-done.71, bf16[192,38,134]{2,1,0:T(8,128)(2,1)} %select_maximum_fusion.2, f32[192]{0:T(256)} %bitcast.50, f32[192]{0:T(256)} %bitcast.49, f32[192]{0:T(256)S(1)} %bitcast.266, bf16[192,3,128]{2,1,0:T(4,128)(2,1)S(1)} %collective-permute-done.1, ...), kind=kLoop, calls=%fused_computation.307 | loop fusion | flops 130543616 | bytes 71128576 | tf_op jit(solution)/shard_map/reduce_sum | solution.py:79
  166.5 2.4 multiply_reduce_fusion
  169.3 7.6 %fusion.7 = (bf16[768,4096]{0,1:T(8,128)(2,1)}, f32[4096,768]{1,0:T(8,128)S(1)}) fusion(f32[768]{0:T(1024)S(1)} %copy-done.72, bf16[192,768]{1,0:T(8,128)(2,1)S(1)} %copy-done, f32[24,8,32,128]{3,2,1,0:T(8,128)S(1)} %bitcast.252, f32[192]{0:T(256)S(1)} %copy-done.73, f32[192]{0:T(256)S(1)} %copy-done.69, f32[4096]{0:T(1024)S(1)} %rsqrt_bitcast_fusion, ...), kind=kOutput, calls=%fused_computation.61 | convolution fusion | flops 1230766080 | bytes 22352384 | tf_op jit(solution)/shard_map/dot_general | solution.py:55
  176.9 6.7 %fusion.5 = bf16[768,4096]{0,1:T(8,128)(2,1)S(1)} fusion(f32[4096,768]{1,0:T(8,128)S(1)} %get-tuple-element.137, bf16[768,192]{0,1:T(8,128)(2,1)S(1)} %copy-done.15, f32[768]{0:T(1024)S(1)} %copy-done.72, f32[192,4096]{1,0:T(8,128)S(1)} %copy-done.6, f32[192]{0:T(256)S(1)} %copy-done.67, f32[4096]{0:T(1024)S(1)} %mul.896), kind=kOutput, calls=%fused_computation.57 | convolution fusion | flops 1244921856 | bytes 22335232 | tf_op jit(solution)/shard_map/dot_general | solution.py:91
  183.6 3.8 fusion.157
  187.5 5.1 %fusion.142 = (f32[4096]{0:T(1024)S(1)}, f32[4096,192]{0,1:T(8,128)}) fusion(f32[24,8,32,128]{3,2,1,0:T(8,128)S(1)} %bitcast.254, f32[4096]{0:T(1024)S(1)} %rsqrt_bitcast_fusion, f32[4096]{0:T(1024)S(1)} %get-tuple-element.134, f32[192]{0:T(256)S(1)} %copy-done.69, bf16[768,4096]{0,1:T(8,128)(2,1)S(1)} %fusion.5, bf16[192,768]{1,0:T(8,128)(2,1)S(1)} %copy-done), kind=kOutput, calls=%fused_computation.257 | convolution fusion | flops 1211887616 | bytes 12927744 | tf_op jit(solution)/shard_map/dot_general | solution.py:93
  192.6 2.0 reduce_sum.48
  194.6 6.1 %fusion.150 = bf16[24,8,32,128]{3,1,2,0:T(8,128)(2,1)S(1)} fusion(f32[24,8,32,128]{3,2,1,0:T(8,128)} %bitcast.251, f32[4096,192]{0,1:T(8,128)} %get-tuple-element.139, f32[4096]{0:T(1024)S(1)} %get-tuple-element.140, f32[4096]{0:T(1024)S(1)} %get-tuple-element.141, f32[4096]{0:T(1024)S(1)} %rsqrt_bitcast_fusion, f32[4096]{0:T(1024)S(1)} %get-tuple-element.134), kind=kLoop, calls=%fused_computation.280 | loop fusion | flops 5505024 | bytes 7929856
  201.1 22.0 %fusion.116 = (f32[192]{0:T(256)}, f32[192]{0:T(256)}, f32[192]{0:T(256)}, f32[192]{0:T(256)}, f32[192]{0:T(256)}, /*index=5*/f32[192]{0:T(256)}, f32[192]{0:T(2...) fusion(bf16[192,38,134]{2,1,0:T(8,128)(2,1)S(1)} %copy-done.2, ...), kind=kLoop, calls=%fused_computation.228 | loop fusion | flops 43250304 | bytes 29898240 | tf_op jit(solution)/shard_map/chw,chw->c/dot_general | solution.py:172
  223.1 22.2 %fusion.137 = (f32[192]{0:T(256)}, f32[192]{0:T(256)}, f32[192]{0:T(256)}, f32[192]{0:T(256)}, f32[192]{0:T(256)}, /*index=5*/f32[192]{0:T(256)}, f32[192]{0:T(2...) fusion(bf16[192,38,134]{2,1,0:T(8,128)(2,1)S(1)} %copy-done.2, ...), kind=kLoop, calls=%fused_computation.249 | loop fusion | flops 43250304 | bytes 29898240 | tf_op jit(solution)/shard_map/chw,chw->c/dot_general | solution.py:172
  245.3 6.3 %fusion.95 = (f32[192]{0:T(256)}, f32[192]{0:T(256)}, f32[192]{0:T(256)}, f32[192]{0:T(256)}, f32[192]{0:T(256)}, /*index=5*/f32[192]{0:T(256)}) fusion(bf16[192,38,134]{2,1,0:T(8,128)(2,1)S(1)} %copy-done.2, bf16[24,8,32,128]{3,2,1,0:T(8,128)(2,1)S(1)} %copy.430), kind=kLoop, calls=%fused_computation.207 | loop fusion | flops 14941056 | bytes 11014656 | tf_op jit(solution)/shard_map/chw,chw->c/dot_general | solution.py:172
  256.7 1.4 copy.144
  261.0 1.4 copy.147
  310.5 7.6 %fusion.134 = (f32[192]{0:T(256)}, f32[192]{0:T(256)}, f32[192]{0:T(256)}, f32[192]{0:T(256)}, f32[192]{0:T(256)}, /*index=5*/f32[192]{0:T(256)}, f32[192]{0:T(256)}) fusion(bf16[192,3,128]{2,1,0:T(4,128)(2,1)} %copy-done.9, bf16[192,32,128]{2,1,0:T(8,128)(2,1)S(1)} %bitcast.259, bf16[24,8,32,128]{3,2,1,0:T(8,128)(2,1)S(1)} %copy.430, ...), kind=kLoop, calls=%fused_computation.246 | loop fusion | flops 31455936 | bytes 5018880 | tf_op jit(solution)/shard_map/chw,chw->c/dot_general | solution.py:172
  328.1 6.1 %fusion.154 = f32[192,768]{1,0:T(8,128)} fusion(bf16[768,4096]{0,1:T(8,128)(2,1)} %get-tuple-element.136, f32[192,4096]{1,0:T(8,128)} %copy.131, f32[192]{0:T(256)} %param.22, f32[4096]{0:T(1024)S(1)} %mul.896), kind=kOutput, calls=%fused_computation.304 | convolution fusion | flops 1210318848 | bytes 10044160 | tf_op jit(solution)/shard_map/dot_general | solution.py:61
  334.8 4.0 concatenate.35
  342.1 4.8 collective-permute-start.2
  346.9 9.0 %fusion.13 = f32[192,4096]{1,0:T(8,128)} fusion(bf16[768,4096]{0,1:T(8,128)(2,1)} %get-tuple-element.136, bf16[768,192]{0,1:T(8,128)(2,1)} %param.20, f32[24,8,32,128]{3,2,1,0:T(8,128)} %convert.150, f32[192]{0:T(256)S(1)} %copy-done.70, f32[192]{0:T(256)S(1)} %copy-done.68, f32[4096]{0:T(1024)S(1)} %mul.896), kind=kOutput, calls=%fused_computation.71 | convolution fusion | flops 1211105280 | bytes 12895744 | tf_op jit(solution)/shard_map/dot_general | solution.py:55
  355.9 5.1 %copy.128 = f32[192,4096]{0,1:T(8,128)} copy(f32[192,4096]{1,0:T(8,128)} %fusion.13) | data formatting | bytes 6291456 | tf_op jit(solution)/shard_map/add | solution.py:89
  361.1 2.6 reduce_sum.47
  364.9 3.4 select_maximum_fusion
  368.4 46.0 %fusion.151 = bf16[1,192,32,128]{3,2,1,0:T(8,128)(2,1)} fusion(bf16[192,38,134]{2,1,0:T(8,128)(2,1)S(1)} %select_maximum_fusion, f32[192]{0:T(256)} %bitcast.50, f32[192]{0:T(256)} %bitcast.49, f32[192]{0:T(256)S(1)} %bitcast.267, bf16[192,32,128]{2,1,0:T(8,128)(2,1)S(1)} %bitcast.250, bf16[192,3,128]{2,1,0:T(4,128)(2,1)S(1)} %collective-permute-done.2, ...), kind=kLoop, calls=%fused_computation.284 | loop fusion | flops 123469824 | bytes 74208000 | tf_op jit(solution)/shard_map/broadcast_in_dim | solution.py:161
  414.5 57.5 %all-reduce.4.cloned.1.call-done = f32[192,1600]{1,0:T(8,128)} async-done(((f32[192,1600]{1,0:T(8,128)}), f32[192,1600]{1,0:T(8,128)}) %all-reduce.4.cloned.1.call-update) | async-done | bytes 1228816 | tf_op jit(solution)/shard_map/psum | solution.py:182
  473.5 2.3 slice_bitcast_fusion
  (231 shorter events, 80.3 us)
Async XLA Ops:
  7.2 161.8 %copy-start = (bf16[192,768]{1,0:T(8,128)(2,1)S(1)}, bf16[192,768]{1,0:T(8,128)(2,1)}, u32[]{:S(2)}) copy-start(bf16[192,768]{1,0:T(8,128)(2,1)} %param.18) | copy-start | bytes 884740
  7.2 464.8 %all-reduce.4.cloned.1.call-start = ((), (), s32[]{:S(2)}) async-start(), calls=%async_computation | async-start | bytes 2555904 | tf_op jit(solution)/shard_map/psum | solution.py:182
  8.6 56.9 %collective-permute-start = (bf16[192,3,128]{2,1,0:T(4,128)(2,1)S(1)}, bf16[192,3,128]{2,1,0:T(4,128)(2,1)S(1)}, u32[]{:S(2)}, u32[]{:S(2)}) collective-permute-start(bf16[192,3,128]{2,1,0:T(4,128)(2,1)S(1)} %get-tuple-element.81), channel_id=1, source_target_pairs={{0,1},{1,2},{2,3},{3,4},{4,5},{5,6},{6,7},{8,9},{9,10},{10,11},{11... | collective-permute-start | bytes 442376 | tf_op jit(solution)/shard_map/ppermute | solution.py:19
  13.5 52.0 %collective-permute-start.1 = (bf16[192,3,128]{2,1,0:T(4,128)(2,1)S(1)}, bf16[192,3,128]{2,1,0:T(4,128)(2,1)S(1)}, u32[]{:S(2)}, u32[]{:S(2)}) collective-permute-start(bf16[192,3,128]{2,1,0:T(4,128)(2,1)S(1)} %get-tuple-element.82), channel_id=1, source_target_pairs={{1,0},{2,1},{3,2},{4,3},{5,4},{6,5},{7,6},{9,8},{10,9},{11,10},{12... | collective-permute-start | bytes 442376 | tf_op jit(solution)/shard_map/ppermute | solution.py:21
  15.9 54.4 %copy-start.16 = (f32[192,1]{0,1:T(1,128)}, f32[192,1]{0,1:T(1,128)S(1)}, u32[]{:S(2)}) copy-start(f32[192,1]{0,1:T(1,128)S(1)} %get-tuple-element.85) | copy-start | bytes 2308
  15.9 54.4 %copy-start.18 = (f32[192,1]{0,1:T(1,128)}, f32[192,1]{0,1:T(1,128)S(1)}, u32[]{:S(2)}) copy-start(f32[192,1]{0,1:T(1,128)S(1)} %get-tuple-element.86) | copy-start | bytes 2308
  15.9 54.4 %copy-start.20 = (f32[192,1]{0,1:T(1,128)}, f32[192,1]{0,1:T(1,128)S(1)}, u32[]{:S(2)}) copy-start(f32[192,1]{0,1:T(1,128)S(1)} %get-tuple-element.87) | copy-start | bytes 2308
  15.9 54.4 %copy-start.22 = (f32[192,1]{0,1:T(1,128)}, f32[192,1]{0,1:T(1,128)S(1)}, u32[]{:S(2)}) copy-start(f32[192,1]{0,1:T(1,128)S(1)} %get-tuple-element.88) | copy-start | bytes 2308
  15.9 54.4 %copy-start.24 = (f32[192,1]{0,1:T(1,128)}, f32[192,1]{0,1:T(1,128)S(1)}, u32[]{:S(2)}) copy-start(f32[192,1]{0,1:T(1,128)S(1)} %get-tuple-element.89) | copy-start | bytes 2308
  15.9 54.4 %copy-start.26 = (f32[192,1]{0,1:T(1,128)}, f32[192,1]{0,1:T(1,128)S(1)}, u32[]{:S(2)}) copy-start(f32[192,1]{0,1:T(1,128)S(1)} %get-tuple-element.90) | copy-start | bytes 2308
  15.9 54.4 %copy-start.28 = (f32[192,1]{0,1:T(1,128)}, f32[192,1]{0,1:T(1,128)S(1)}, u32[]{:S(2)}) copy-start(f32[192,1]{0,1:T(1,128)S(1)} %get-tuple-element.91) | copy-start | bytes 2308
  15.9 54.4 %copy-start.30 = (f32[192,1]{0,1:T(1,128)}, f32[192,1]{0,1:T(1,128)S(1)}, u32[]{:S(2)}) copy-start(f32[192,1]{0,1:T(1,128)S(1)} %get-tuple-element.92) | copy-start | bytes 2308
  15.9 54.4 %copy-start.32 = (f32[192,1]{0,1:T(1,128)}, f32[192,1]{0,1:T(1,128)S(1)}, u32[]{:S(2)}) copy-start(f32[192,1]{0,1:T(1,128)S(1)} %get-tuple-element.93) | copy-start | bytes 2308
  15.9 54.4 %copy-start.34 = (f32[192,1]{0,1:T(1,128)}, f32[192,1]{0,1:T(1,128)S(1)}, u32[]{:S(2)}) copy-start(f32[192,1]{0,1:T(1,128)S(1)} %get-tuple-element.94) | copy-start | bytes 2308
  16.0 54.4 %copy-start.36 = (f32[192,1]{0,1:T(1,128)}, f32[192,1]{0,1:T(1,128)S(1)}, u32[]{:S(2)}) copy-start(f32[192,1]{0,1:T(1,128)S(1)} %get-tuple-element.95) | copy-start | bytes 2308
  16.0 54.4 %copy-start.38 = (f32[192,1]{0,1:T(1,128)}, f32[192,1]{0,1:T(1,128)S(1)}, u32[]{:S(2)}) copy-start(f32[192,1]{0,1:T(1,128)S(1)} %get-tuple-element.96) | copy-start | bytes 2308
  16.0 54.4 %copy-start.40 = (f32[192,1]{0,1:T(1,128)}, f32[192,1]{0,1:T(1,128)S(1)}, u32[]{:S(2)}) copy-start(f32[192,1]{0,1:T(1,128)S(1)} %get-tuple-element.97) | copy-start | bytes 2308
  16.0 54.4 %copy-start.42 = (f32[192,1]{0,1:T(1,128)}, f32[192,1]{0,1:T(1,128)S(1)}, u32[]{:S(2)}) copy-start(f32[192,1]{0,1:T(1,128)S(1)} %get-tuple-element.98) | copy-start | bytes 2308
  16.0 54.4 %copy-start.44 = (f32[192,1]{0,1:T(1,128)}, f32[192,1]{0,1:T(1,128)S(1)}, u32[]{:S(2)}) copy-start(f32[192,1]{0,1:T(1,128)S(1)} %get-tuple-element.99) | copy-start | bytes 2308
  16.0 54.4 %copy-start.45 = (f32[192,1]{0,1:T(1,128)}, f32[192,1]{0,1:T(1,128)S(1)}, u32[]{:S(2)}) copy-start(f32[192,1]{0,1:T(1,128)S(1)} %get-tuple-element.100) | copy-start | bytes 2308
  16.0 54.4 %copy-start.46 = (f32[192,1]{0,1:T(1,128)}, f32[192,1]{0,1:T(1,128)S(1)}, u32[]{:S(2)}) copy-start(f32[192,1]{0,1:T(1,128)S(1)} %get-tuple-element.101) | copy-start | bytes 2308
  16.0 54.4 %copy-start.47 = (f32[192,1]{0,1:T(1,128)}, f32[192,1]{0,1:T(1,128)S(1)}, u32[]{:S(2)}) copy-start(f32[192,1]{0,1:T(1,128)S(1)} %get-tuple-element.102) | copy-start | bytes 2308
  16.0 54.4 %copy-start.48 = (f32[192,1]{0,1:T(1,128)}, f32[192,1]{0,1:T(1,128)S(1)}, u32[]{:S(2)}) copy-start(f32[192,1]{0,1:T(1,128)S(1)} %get-tuple-element.103) | copy-start | bytes 2308
  17.7 52.8 %copy-start.51 = (f32[192,1]{0,1:T(1,128)}, f32[192,1]{0,1:T(1,128)S(1)}, u32[]{:S(2)}) copy-start(f32[192,1]{0,1:T(1,128)S(1)} %get-tuple-element.106) | copy-start | bytes 2308
  17.7 52.8 %copy-start.52 = (f32[192,1]{0,1:T(1,128)}, f32[192,1]{0,1:T(1,128)S(1)}, u32[]{:S(2)}) copy-start(f32[192,1]{0,1:T(1,128)S(1)} %get-tuple-element.107) | copy-start | bytes 2308
  65.5 101.0 %copy-start.7 = (bf16[192,3,128]{2,1,0:T(4,128)(2,1)}, bf16[192,3,128]{2,1,0:T(4,128)(2,1)S(1)}, u32[]{:S(2)}) copy-start(bf16[192,3,128]{2,1,0:T(4,128)(2,1)S(1)} %collective-permute-done) | copy-start | bytes 442372
  65.5 100.9 %copy-start.9 = (bf16[192,3,128]{2,1,0:T(4,128)(2,1)}, bf16[192,3,128]{2,1,0:T(4,128)(2,1)S(1)}, u32[]{:S(2)}) copy-start(bf16[192,3,128]{2,1,0:T(4,128)(2,1)S(1)} %collective-permute-done.1) | copy-start | bytes 442372
  251.6 58.9 %copy-start.5 = (bf16[1,192,32,128]{3,2,1,0:T(8,128)(2,1)S(1)}, bf16[1,192,32,128]{3,2,1,0:T(8,128)(2,1)}, u32[]{:S(2)}) copy-start(bf16[1,192,32,128]{3,2,1,0:T(8,128)(2,1)} %param.13) | copy-start | bytes 4718596
  251.6 58.9 %copy-start.8 = (bf16[192,3,128]{2,1,0:T(4,128)(2,1)S(1)}, bf16[192,3,128]{2,1,0:T(4,128)(2,1)}, u32[]{:S(2)}) copy-start(bf16[192,3,128]{2,1,0:T(4,128)(2,1)} %copy-done.7) | copy-start | bytes 442372
  340.8 23.9 %collective-permute-start.3 = (bf16[192,3,128]{2,1,0:T(4,128)(2,1)}, bf16[192,3,128]{2,1,0:T(4,128)(2,1)S(1)}, u32[]{:S(2)}, u32[]{:S(2)}) collective-permute-start(bf16[192,3,128]{2,1,0:T(4,128)(2,1)} %get-tuple-element.80), channel_id=1, source_target_pairs={{1,0},{2,1},{3,2},{4,3},{5,4},{6,5},{7,6},{9,8},{10,9},{11,10},{12... | collective-permute-start | bytes 442376 | tf_op jit(solution)/shard_map/ppermute | solution.py:21
  342.1 22.7 %collective-permute-start.2 = (bf16[192,3,128]{2,1,0:T(4,128)(2,1)S(1)}, bf16[192,3,128]{2,1,0:T(4,128)(2,1)S(1)}, u32[]{:S(2)}, u32[]{:S(2)}) collective-permute-start(bf16[192,3,128]{2,1,0:T(4,128)(2,1)S(1)} %get-tuple-element.79), channel_id=1, source_target_pairs={{0,1},{1,2},{2,3},{3,4},{4,5},{5,6},{6,7},{8,9},{9,10},{10,11},{11... | collective-permute-start | bytes 442376 | tf_op jit(solution)/shard_map/ppermute | solution.py:19
  368.4 107.5 %copy-start.1 = (bf16[192,768]{1,0:T(8,128)(2,1)S(1)}, bf16[192,768]{1,0:T(8,128)(2,1)}, u32[]{:S(2)}) copy-start(bf16[192,768]{1,0:T(8,128)(2,1)} %param.18) | copy-start | bytes 884740
  (48 other events, 1004.5 us)
Sparse Core Ops, SparseCore 0:
  340.1 131.7 all-reduce.3
where the time goes:
time: 493 us; the launch traced here: 483 us
  other arithmetic  227 us (46%)
  local copies, waits for them, and re-layouts  99.7 us (20%)
  waiting for transfers between devices  57.5 us (12%)
  matrix products  38.3 us (8%)
  blocking collectives  32.9 us (7%)
  between operations  15.7 us (3%)
  starting transfers between devices  12.3 us (2%)
    reduce_sum x1, other arithmetic, block_pass(): average = jnp.mean(conv_flat, axis=0, keepdims=True)  95.8 us
    another operation x49, local copies, waits for them, and re-layouts, on_device(): kernel_term = jnp.stack(kernel_cols, axis=1)  68.8 us
    dot_general x4, other arithmetic, on_device(): jnp.einsum('chw,chw->c', grad_image, window, preferred_element_type=jnp.f...  58.1 us
    psum x1, waiting for transfers between devices, on_device(): totals = lax.psum(combined, ('slide', 'rows'))  57.5 us
    broadcast_in_dim x1, other arithmetic, on_device(): (pixel_cotangent.reshape(channels, height, across) + backward_conv).astyp...  46 us
    all_gather x1, blocking collectives, on_device(): gathered = lax.all_gather(tile_cotangent, 'rows', axis=1, tiled=True)[0]  32.9 us
    dot_general x2, matrix products, contract_first(): lax.dot_general(left, right, (((0,), (0,)), ((), ())), preferred_element_...  16.6 us
    dot_general x2, matrix products, contract_last(): lax.dot_general(left, right, (((1,), (1,)), ((), ())), preferred_element_...  9.9 us
  transfers between devices with their start and end apart: 5, of which 1 were waited for; matrix products, arithmetic and copies ran while one was open for 18% of the time, Pallas kernels for 0%

commit v1 on v0

v1 whole, which is shorter than its diff:
```python
import math

import jax
import jax.numpy as jnp
from jax import lax
from jax.experimental import pallas as pl
from jax.experimental.pallas import tpu as pltpu
from jax.sharding import PartitionSpec as P

TILE = 32
SLOT = 40
PER = 3
ROWS = 4
VMEM = pl.BlockSpec(memory_space=pltpu.VMEM)


def extended_rows(cells, axis):
    channels, height, across = cells.shape
    count = lax.axis_size(axis)
    above = lax.ppermute(cells[:, height - 3 :], axis, [(i, i + 1) for i in range(count - 1)])
    below = lax.ppermute(cells[:, :3], axis, [(i + 1, i) for i in range(count - 1)])
    spare = jnp.zeros((channels, SLOT - height - 6, across), cells.dtype)
    return jnp.concatenate([above, cells, below, spare], axis=1)


def shifted_stack(rows):
    across = rows.shape[1]
    lane = lax.broadcasted_iota(jnp.int32, rows.shape, 1)
    spare = jnp.zeros((across - PER * SLOT, across), jnp.float32)
    pieces = []
    for b in range(7):
        offset = b - 3
        if offset == 0:
            piece = rows
        else:
            piece = pltpu.roll(rows, (-offset) % across, 1)
            inside = lane < across - offset if offset > 0 else lane >= -offset
            piece = jnp.where(inside, piece, 0.0)
        pieces.append(piece)
        if b % PER == PER - 1:
            pieces.append(spare)
    return jnp.concatenate(pieces, axis=0).astype(jnp.bfloat16)


def banded(taps_ref, c, height):
    parts = []
    for g in range(3):
        part = jnp.broadcast_to(taps_ref[g, pl.ds(c, 1), :], (height, 128))
        parts.append(pltpu.roll(part, 0, 1, stride=1, stride_axis=0))
    return jnp.concatenate(parts, axis=1)


def diagonal_sums(cells):
    height, across = cells.shape
    total = cells[:8]
    for start in range(8, height, 8):
        total = total + pltpu.roll(cells[start : start + 8], across - start, 1)
    row = lax.broadcasted_iota(jnp.int32, total.shape, 0)
    for bit in (4, 2, 1):
        total = jnp.where((row // bit) % 2 == 1, pltpu.roll(total, across - bit, 1), total)
    return jnp.sum(total, axis=0, keepdims=True)


def forward_kernel(
    ext_ref, taps_hi, taps_lo, conv_bias, gain_ref, bias_ref, up_ref, up_bias, down_ref,
    down_bias, mask_ref, branch_ref,
    grad_ref, embed_ref, up_out, down_out, held, sums, hidden_sum, slope_gain,
):
    channels, _, across = ext_ref.shape
    height = grad_ref.shape[1]
    hidden_units = up_ref.shape[1]
    depth = 2 * 128 + SLOT

    def conv_channel(c, carry):
        rows = ext_ref[c].astype(jnp.float32)
        stack = shifted_stack(rows)
        hi = banded(taps_hi, c, height)
        lo = banded(taps_lo, c, height)
        left = jnp.concatenate([hi, lo], axis=0).astype(jnp.bfloat16)[:, :depth]
        both = jnp.dot(left, stack, preferred_element_type=jnp.float32)
        held[pl.ds(c, height, stride=channels), :] = both[:height] + both[height:]
        sums[pl.ds(c, 1), :] = jnp.sum(rows, axis=0, keepdims=True) - jnp.sum(
            rows[:3], axis=0, keepdims=True
        ) - jnp.sum(rows[height + 3 :], axis=0, keepdims=True)
        return carry

    lax.fori_loop(0, channels, conv_channel, 0, unroll=4)

    slope_gain[...] = jnp.dot(down_ref[...], branch_ref[...], preferred_element_type=jnp.float32)
    hidden_sum[...] = jnp.zeros_like(hidden_sum)
    up_out[...] = jnp.zeros_like(up_out)

    def pixels(block, carry):
        parts = []
        for r in range(ROWS):
            start = pl.multiple_of((block * ROWS + r) * channels, 8)
            parts.append(held[pl.ds(start, channels), :])
        conv = jnp.concatenate(parts, axis=1) + conv_bias[...]
        average = jnp.mean(conv, axis=0, keepdims=True)
        centered = conv - average
        variance = jnp.mean(centered * centered, axis=0, keepdims=True)
        reciprocal = lax.rsqrt(variance + 1e-06)
        standard = centered * reciprocal
        normed = (standard * gain_ref[...] + bias_ref[...]).astype(jnp.bfloat16)
        act = lax.dot_general(
            up_ref[...], normed, (((0,), (0,)), ((), ())), preferred_element_type=jnp.float32
        )
        act = act + up_bias[...]
        cumulative = 0.5 + 0.5 * lax.erf(act * 0.7071067811865476)
        hidden = (act * cumulative).astype(jnp.bfloat16).astype(jnp.float32)
        total = hidden_sum[...]
        for r in range(ROWS):
            total = total + hidden[:, r * across : (r + 1) * across]
        hidden_sum[...] = total
        density = jnp.exp(-0.5 * act * act) * 0.3989422804014327
        slope = cumulative + act * density
        grad_hidden = jnp.concatenate([slope_gain[...]] * ROWS, axis=1)
        grad_act = (grad_hidden * slope).astype(jnp.bfloat16)
        grad_normed = jnp.dot(up_ref[...], grad_act, preferred_element_type=jnp.float32)
        up_out[...] += lax.dot_general(
            normed, grad_act, (((1,), (1,)), ((), ())), preferred_element_type=jnp.float32
        )
        grad_standard = grad_normed * gain_ref[...]
        first = jnp.mean(grad_standard, axis=0, keepdims=True)
        second = jnp.mean(grad_standard * standard, axis=0, keepdims=True)
        grad_conv = reciprocal * (grad_standard - first - standard * second)
        for r in range(ROWS):
            start = pl.multiple_of((block * ROWS + r) * channels, 8)
            held[pl.ds(start, channels), :] = grad_conv[:, r * across : (r + 1) * across]
        return carry

    lax.fori_loop(0, height // ROWS, pixels, 0)

    total = hidden_sum[...]
    total_hi = total.astype(jnp.bfloat16)
    total_lo = (total - total_hi.astype(jnp.float32)).astype(jnp.bfloat16)
    branch = jnp.zeros((channels, across), jnp.float32)
    down = jnp.zeros((channels, hidden_units), jnp.float32)
    for part in (total_hi, total_lo):
        branch += lax.dot_general(
            down_ref[...], part, (((0,), (0,)), ((), ())), preferred_element_type=jnp.float32
        )
        down += lax.dot_general(
            branch_ref[...], part, (((1,), (1,)), ((), ())), preferred_element_type=jnp.float32
        )
    down_out[...] = down
    embed_ref[...] = sums[...] + mask_ref[...] * (branch + height * down_bias[...])

    def turn(c, carry):
        grad_ref[c] = held[pl.ds(c, height, stride=channels), :].astype(jnp.bfloat16)
        return carry

    lax.fori_loop(0, channels, turn, 0, unroll=8)


def backward_kernel(grad_ref, image_ref, taps_ref, cotangent_ref, out_ref, kernel_ref):
    channels, height, across = image_ref.shape
    depth = 2 * 128 + SLOT

    def channel(c, carry):
        stack = shifted_stack(grad_ref[c].astype(jnp.float32))
        left = banded(taps_ref, c, height).astype(jnp.bfloat16)[:, :depth]
        conv = jnp.dot(left, stack, preferred_element_type=jnp.float32)
        out_ref[c] = (conv + cotangent_ref[pl.ds(c, 1), :]).astype(jnp.bfloat16)
        spare = jnp.zeros((3 * 128 - depth, across), jnp.bfloat16)
        cross = lax.dot_general(
            image_ref[c],
            jnp.concatenate([stack, spare], axis=0),
            (((1,), (1,)), ((), ())),
            preferred_element_type=jnp.float32,
        )
        for g in range(3):
            kernel_ref[g, pl.ds(c, 1), :] = diagonal_sums(cross[:, g * 128 : (g + 1) * 128])
        return carry

    lax.fori_loop(0, channels, channel, 0, unroll=4)


def tap_rows(taps):
    channels = taps.shape[0]
    by_column = jnp.pad(taps.transpose(0, 2, 1), ((0, 0), (0, 2), (0, SLOT - 7)))
    groups = by_column.reshape(channels, 3, PER * SLOT)
    return jnp.pad(groups, ((0, 0), (0, 0), (0, 128 - PER * SLOT))).transpose(1, 0, 2)


def taps_of(rows):
    channels = rows.shape[1]
    groups = rows[:, :, : PER * SLOT].transpose(1, 0, 2).reshape(channels, 9, SLOT)
    return groups[:, :7, :7].transpose(0, 2, 1)


def on_device(
    features,
    depth_kernel,
    depth_bias,
    norm_gain,
    norm_bias,
    up_weight,
    up_bias,
    down_weight,
    down_bias,
    layer_scale,
    tissue,
    aggregator_order,
    tile_cotangent,
):
    image = features[0]
    channels, height, across = image.shape
    tiles_here = across // TILE
    hidden_units = up_weight.shape[1]
    taps = depth_kernel.reshape(channels, 7, 7)
    rows = tap_rows(taps)
    rows_hi = lax.reduce_precision(rows, 8, 7)
    rows_lo = rows - rows_hi
    rows_back = tap_rows(taps[:, ::-1, ::-1])
    gathered = lax.all_gather(tile_cotangent, "rows", axis=1, tiled=True)[0]
    positions = lax.dynamic_slice_in_dim(
        aggregator_order[0], lax.axis_index("rows") * tiles_here, tiles_here
    )
    wanted = jnp.take(gathered, positions, axis=0).astype(jnp.float32)
    cotangent = jnp.repeat(wanted.T, TILE, axis=1)
    mask = jnp.repeat(tissue[0, 0].astype(jnp.float32), TILE)
    scaled_mask = mask[None, :] * layer_scale[:, None]
    grad_branch = (scaled_mask * cotangent).astype(jnp.bfloat16)
    f32 = jnp.float32
    grad_conv, embed, up_term, down_term = pl.pallas_call(
        forward_kernel,
        out_shape=(
            jax.ShapeDtypeStruct((channels, height, across), jnp.bfloat16),
            jax.ShapeDtypeStruct((channels, across), f32),
            jax.ShapeDtypeStruct((channels, hidden_units), f32),
            jax.ShapeDtypeStruct((channels, hidden_units), f32),
        ),
        in_specs=[VMEM] * 12,
        out_specs=(VMEM,) * 4,
        scratch_shapes=[
            pltpu.VMEM((height * channels, across), f32),
            pltpu.VMEM((channels, across), f32),
            pltpu.VMEM((hidden_units, across), f32),
            pltpu.VMEM((hidden_units, across), f32),
        ],
        compiler_params=pltpu.CompilerParams(vmem_limit_bytes=56 * 1024 * 1024),
        name="forward_block",
    )(
        extended_rows(image, "rows"),
        rows_hi,
        rows_lo,
        depth_bias[:, None],
        norm_gain[:, None],
        norm_bias[:, None],
        up_weight,
        up_bias[:, None],
        down_weight,
        down_bias[:, None],
        scaled_mask,
        grad_branch,
    )
    embedding = (
        embed.reshape(channels, tiles_here, TILE).sum(axis=2) / (height * TILE)
    ).T[None]
    input_grad, kernel_rows = pl.pallas_call(
        backward_kernel,
        out_shape=(
            jax.ShapeDtypeStruct((channels, height, across), jnp.bfloat16),
            jax.ShapeDtypeStruct((3, channels, 128), f32),
        ),
        in_specs=[VMEM] * 4,
        out_specs=(VMEM,) * 2,
        compiler_params=pltpu.CompilerParams(vmem_limit_bytes=40 * 1024 * 1024),
        name="backward_conv",
    )(extended_rows(grad_conv, "rows"), image, rows_back, cotangent)
    kernel_term = taps_of(kernel_rows)[:, ::-1, ::-1].reshape(channels, 49)
    loss_norm = 1.0 / math.sqrt(lax.axis_size("slide") * lax.axis_size("rows") * height * across)
    combined = (
        jnp.concatenate(
            [up_term, down_term, kernel_term, jnp.zeros((channels, 15), f32)], axis=1
        )
        * loss_norm
    )
    totals = lax.psum(combined, ("slide", "rows"))
    grad_up = totals[:, :hidden_units]
    grad_down = totals[:, hidden_units : 2 * hidden_units].T
    grad_kernel = totals[:, 2 * hidden_units : 2 * hidden_units + 49]
    return (embedding, input_grad[None], grad_up, grad_down, grad_kernel)


def solution(mesh):
    return jax.shard_map(
        on_device,
        mesh=mesh,
        in_specs=(
            P("slide", None, "rows", None),
            P(),
            P(),
            P(),
            P(),
            P(),
            P(),
            P(),
            P(),
            P(),
            P("slide", "rows", None),
            P("slide", None),
            P("slide", "rows", None),
        ),
        out_specs=(P("slide", "rows", None), P("slide", None, "rows", None), P(), P(), P()),
        check_vma=False,
    )
```

time: 493 us -> 290 us (0.59); the launches traced: 483 us -> 290 us
  other arithmetic: 227 us -> 11.1 us
  local copies, waits for them, and re-layouts: 99.7 us -> 19.3 us
  waiting for transfers between devices: 57.5 us -> 135 us
  Pallas kernels: 0 us -> 66.4 us
  matrix products: 38.3 us -> 0 us
    reduce_sum x4 -> x1, other arithmetic: 103 us -> 0.03 us  [on_device(): embed.reshape(channels, tiles_here, TILE).sum(axis=2) / (height * TILE)]
    psum x1, waiting for transfers between devices: 57.5 us -> 130 us  [on_device(): totals = lax.psum(combined, ('slide', 'rows'))]
    another operation x49 -> x1, local copies, waits for them, and re-layouts: 68.8 us -> 0.01 us  [on_device(): kernel_term = jnp.stack(kernel_cols, axis=1)]
    pallas_call x0 -> x2, Pallas kernels: none -> 66.4 us  [the longest x1 35 us: on_device(): pl.pallas_call(forward_kernel, out_shape=(jax.ShapeDtypeStruct((channels,...]
    dot_general x4 -> x0, other arithmetic: 58.1 us -> none  [on_device(): jnp.einsum('chw,chw->c', grad_image, window, preferred_element_type=jnp.f...]
    broadcast_in_dim x2 -> x1, other arithmetic: 46.6 us -> 0.6 us  [on_device(): (embed.reshape(channels, tiles_here, TILE).sum(axis=2) / (height * TILE))...]
    dot_general x6 -> x0, matrix products: 38.3 us -> none  [the longest x2 16.6 us: contract_first(): lax.dot_general(left, right, (((0,), (0,)), ((), ())), preferred_element_...]
    unnamed x2 -> x0, other arithmetic: 8.23 us -> none
  transfers between devices with their start and end apart: 5 -> 5, of which waited for: 1 -> 2; matrix products, arithmetic and copies ran while one was open for 18% -> 5% of each run, Pallas kernels for 0% -> 0%
where the time goes in v1:
time: 290 us
  waiting for transfers between devices  135 us (47%)
  Pallas kernels  66.4 us (23%)
  blocking collectives  32.9 us (11%)
  local copies, waits for them, and re-layouts  19.3 us (7%)
  between operations  14.3 us (5%)
  other arithmetic  11.1 us (4%)
  starting transfers between devices  10.7 us (4%)
    psum x1, waiting for transfers between devices, on_device(): totals = lax.psum(combined, ('slide', 'rows'))  130 us
    pallas_call x1, Pallas kernels, on_device(): pl.pallas_call(forward_kernel, out_shape=(jax.ShapeDtypeStruct((channels,...  35 us
    all_gather x1, blocking collectives, on_device(): gathered = lax.all_gather(tile_cotangent, 'rows', axis=1, tiled=True)[0]  32.9 us
    pallas_call x1, Pallas kernels, on_device(): pl.pallas_call(backward_kernel, out_shape=(jax.ShapeDtypeStruct((channels...  31.4 us
    ppermute x2, starting transfers between devices, extended_rows(): lax.ppermute(cells[:, height - 3:], axis, [(i, i + 1) for i in range(coun...  8.12 us
  transfers between devices with their start and end apart: 5, of which 2 were waited for; matrix products, arithmetic and copies ran while one was open for 5% of the time, Pallas kernels for 0%

profile of v1, /device:TPU:0, one launch (start us, length us, event | category | flops | bytes accessed | tf_op | source)
XLA Modules:
  0.0 289.8 jit_solution(12014340703531438104)
XLA Ops:
  7.3 2.0 fusion.2
  9.3 4.9 %collective-permute-start = (bf16[192,3,128]{2,1,0:T(4,128)(2,1)}, bf16[192,3,128]{2,1,0:T(4,128)(2,1)S(1)}, u32[]{:S(2)}, u32[]{:S(2)}) collective-permute-start(bf16[192,3,128]{2,1,0:T(4,128)(2,1)} %get-tuple-element.39), channel_id=1, source_target_pairs={{0,1},{1,2},{2,3},{3,4},{4,5},{5,6},{6,7},{8,9},{9,10},{10,11},{11... | collective-permute-start | bytes 442376 | tf_op jit(solution)/shard_map/ppermute | solution.py:20
  14.2 1.3 collective-permute-start.1
  15.5 0.7 fusion
  16.2 0.7 compare_and_fusion
  17.0 0.7 copy.58
  17.7 32.9 %all_gather.3 = bf16[1,32,192]{2,0,1:T(2,128)(2,1)S(1)} all-gather(bf16[1,4,192]{2,0,1:T(2,128)(2,1)S(1)} %copy.58), channel_id=1, replica_groups=mesh['slide'=4,'rows'=8] {'rows'}, dimensions={1}, use_global_device_ids=true | all-gather | bytes 13824 | tf_op jit(solution)/shard_map/all_gather | solution.py:216
  51.4 0.7 convert_bitcast_fusion.1
  52.2 1.5 multiply_convert_fusion
  53.7 0.8 reshape.69
  54.8 0.9 broadcast_in_dim.53.up_bias
  55.7 0.9 copy.64.down_ref
  56.7 0.8 copy.60.conv_bias
  57.4 0.8 copy.61.gain_ref
  58.2 0.8 copy.62.bias_ref
  59.0 0.8 copy.65.down_bias
  59.8 0.9 bitcast_subtract_fusion
  60.7 2.5 maximum_maximum_fusion.ext_ref
  63.2 35.0 %forward_block.1 = (bf16[192,32,128]{2,1,0:T(8,128)(2,1)}, f32[192,128]{1,0:T(8,128)}, f32[192,768]{1,0:T(8,128)}, f32[192,768]{1,0:T(8,128)}) custom-call(bf16[192,40,128]{2,1,0:T(8,128)(2,1)} %maximum_maximum_fusion.ext_ref, f32[3,192,128]{2,1,0:T(8,128)} %get-tuple-element.44.taps_hi, f32[3,192,128]{2,1,0:T(8,128)} %get-tuple-element.43.taps_lo, ...), custom_call_target="tpu_custom_call" | custom-call | tf_op jit(solution)/shard_map/forward_block/pallas_call | solution.py:226
  98.2 2.2 fusion.1
  100.3 3.2 %collective-permute-start.2 = (bf16[192,3,128]{2,1,0:T(4,128)(2,1)}, bf16[192,3,128]{2,1,0:T(4,128)(2,1)}, u32[]{:S(2)}, u32[]{:S(2)}) collective-permute-start(bf16[192,3,128]{2,1,0:T(4,128)(2,1)} %get-tuple-element.37), channel_id=1, source_target_pairs={{0,1},{1,2},{2,3},{3,4},{4,5},{5,6},{6,7},{8,9},{9,10},{10,11},{11... | collective-permute-start | bytes 442376 | tf_op jit(solution)/shard_map/ppermute | solution.py:20
  103.5 1.3 collective-permute-start.3
  104.9 0.8 pad.16
  105.7 1.1 copy.68
  106.9 4.5 %collective-permute-done.3 = bf16[192,3,128]{2,1,0:T(4,128)(2,1)} collective-permute-done((bf16[192,3,128]{2,1,0:T(4,128)(2,1)}, bf16[192,3,128]{2,1,0:T(4,128)(2,1)}, u32[]{:S(2)}, u32[]{:S(2)}) %collective-permute-start.3) | collective-permute-done | bytes 147488 | tf_op jit(solution)/shard_map/ppermute | solution.py:21
  111.4 2.2 maximum_maximum_fusion.1.grad_ref
  113.7 31.4 %backward_conv.1 = (bf16[192,32,128]{2,1,0:T(8,128)(2,1)}, f32[3,192,128]{2,1,0:T(8,128)S(1)}) custom-call(bf16[192,40,128]{2,1,0:T(8,128)(2,1)S(1)} %maximum_maximum_fusion.1.grad_ref, bf16[192,32,128]{2,1,0:T(8,128)(2,1)S(1)} %bitcast.51, f32[3,192,128]{2,1,0:T(8,128)S(1)} %pad_bitcast_fusion.taps_ref, f32[192,128]{1,0:T(8,128)S(1)} %copy.59.cotangent_ref), custom_call_target="tpu_custom_call" | custom-call | tf_op jit(solution)/shard_map/backward_conv/pallas_call | solution.py:261
  146.6 1.2 broadcast_multiply_fusion
  148.5 130.5 %all-reduce.6.cloned.1.call-done = f32[192,1600]{1,0:T(8,128)} async-done(((f32[192,1600]{1,0:T(8,128)}), f32[192,1600]{1,0:T(8,128)}) %all-reduce.6.cloned.1.call-update) | async-done | bytes 1228816 | tf_op jit(solution)/shard_map/psum | solution.py:280
  279.0 0.9 slice.43
  279.9 0.7 copy.73
  280.6 2.3 slice_bitcast_fusion
  (54 shorter events, 3.6 us)
Async XLA Ops:
  7.2 47.6 %copy-start.6 = (f32[768]{0:T(1024)S(1)}, f32[768]{0:T(1024)}, u32[]{:S(2)}) copy-start(f32[768]{0:T(1024)} %param.19) | copy-start | bytes 9220
  7.2 48.5 %copy-start.4 = (bf16[768,192]{0,1:T(8,128)(2,1)S(1)}, bf16[768,192]{0,1:T(8,128)(2,1)}, u32[]{:S(2)}) copy-start(bf16[768,192]{0,1:T(8,128)(2,1)} %param.20) | copy-start | bytes 884740
  7.2 271.8 %all-reduce.6.cloned.1.call-start = ((), (), s32[]{:S(2)}) async-start(), calls=%async_computation | async-start | bytes 2555904 | tf_op jit(solution)/shard_map/psum | solution.py:280
  7.2 49.4 %copy-start.7 = (f32[192]{0:T(256)S(1)}, f32[192]{0:T(256)}, u32[]{:S(2)}) copy-start(f32[192]{0:T(256)} %param.15) | copy-start | bytes 2308
  7.2 50.2 %copy-start.8 = (f32[192]{0:T(256)S(1)}, f32[192]{0:T(256)}, u32[]{:S(2)}) copy-start(f32[192]{0:T(256)} %param.16) | copy-start | bytes 2308
  7.3 51.0 %copy-start.9 = (f32[192]{0:T(256)S(1)}, f32[192]{0:T(256)}, u32[]{:S(2)}) copy-start(f32[192]{0:T(256)} %param.17) | copy-start | bytes 2308
  7.3 51.7 %copy-start.10 = (f32[192]{0:T(256)S(1)}, f32[192]{0:T(256)}, u32[]{:S(2)}) copy-start(f32[192]{0:T(256)} %param.21) | copy-start | bytes 2308
  9.3 51.4 %collective-permute-start = (bf16[192,3,128]{2,1,0:T(4,128)(2,1)}, bf16[192,3,128]{2,1,0:T(4,128)(2,1)S(1)}, u32[]{:S(2)}, u32[]{:S(2)}) collective-permute-start(bf16[192,3,128]{2,1,0:T(4,128)(2,1)} %get-tuple-element.39), channel_id=1, source_target_pairs={{0,1},{1,2},{2,3},{3,4},{4,5},{5,6},{6,7},{8,9},{9,10},{10,11},{11... | collective-permute-start | bytes 442376 | tf_op jit(solution)/shard_map/ppermute | solution.py:20
  14.2 46.5 %collective-permute-start.1 = (bf16[192,3,128]{2,1,0:T(4,128)(2,1)S(1)}, bf16[192,3,128]{2,1,0:T(4,128)(2,1)S(1)}, u32[]{:S(2)}, u32[]{:S(2)}) collective-permute-start(bf16[192,3,128]{2,1,0:T(4,128)(2,1)S(1)} %get-tuple-element.40), channel_id=1, source_target_pairs={{1,0},{2,1},{3,2},{4,3},{5,4},{6,5},{7,6},{9,8},{10,9},{11,10},{12... | collective-permute-start | bytes 442376 | tf_op jit(solution)/shard_map/ppermute | solution.py:21
  52.2 8.5 %copy-start = (bf16[1,192,32,128]{3,2,1,0:T(8,128)(2,1)S(1)}, bf16[1,192,32,128]{3,2,1,0:T(8,128)(2,1)}, u32[]{:S(2)}) copy-start(bf16[1,192,32,128]{3,2,1,0:T(8,128)(2,1)} %param.13) | copy-start | bytes 4718596
  98.2 13.3 %copy-start.1 = (bf16[192,32,128]{2,1,0:T(8,128)(2,1)S(1)}, bf16[192,32,128]{2,1,0:T(8,128)(2,1)}, u32[]{:S(2)}) copy-start(bf16[192,32,128]{2,1,0:T(8,128)(2,1)} %get-tuple-element.12) | copy-start | bytes 4718596
  100.3 6.6 %collective-permute-start.2 = (bf16[192,3,128]{2,1,0:T(4,128)(2,1)}, bf16[192,3,128]{2,1,0:T(4,128)(2,1)}, u32[]{:S(2)}, u32[]{:S(2)}) collective-permute-start(bf16[192,3,128]{2,1,0:T(4,128)(2,1)} %get-tuple-element.37), channel_id=1, source_target_pairs={{0,1},{1,2},{2,3},{3,4},{4,5},{5,6},{6,7},{8,9},{9,10},{10,11},{11... | collective-permute-start | bytes 442376 | tf_op jit(solution)/shard_map/ppermute | solution.py:20
  103.5 7.9 %collective-permute-start.3 = (bf16[192,3,128]{2,1,0:T(4,128)(2,1)}, bf16[192,3,128]{2,1,0:T(4,128)(2,1)}, u32[]{:S(2)}, u32[]{:S(2)}) collective-permute-start(bf16[192,3,128]{2,1,0:T(4,128)(2,1)} %get-tuple-element.38), channel_id=1, source_target_pairs={{1,0},{2,1},{3,2},{4,3},{5,4},{6,5},{7,6},{9,8},{10,9},{11,10},{12... | collective-permute-start | bytes 442376 | tf_op jit(solution)/shard_map/ppermute | solution.py:21
  145.0 1.1 copy-start.2
  145.0 1.2 copy-start.3
  146.6 1.2 copy-start.5
Sparse Core Ops, SparseCore 0:
  147.9 131.0 all-reduce.5

commit v2 on v1

--- a/solution.py
+++ b/solution.py
@@ -1,3 +1,4 @@
+import functools
 import math
 
 import jax
@@ -11,16 +12,146 @@
 SLOT = 40
 PER = 3
 ROWS = 4
+MESH = pl.DeviceIdType.MESH
 VMEM = pl.BlockSpec(memory_space=pltpu.VMEM)
 
 
-def extended_rows(cells, axis):
+def greet(peers):
+    barrier = pltpu.get_barrier_semaphore()
+    for peer in peers:
+        pl.semaphore_signal(barrier, inc=1, device_id=peer, device_id_type=MESH)
+    pl.semaphore_wait(barrier, len(peers))
+
+
+def remote(source, target, send, receive, peer):
+    copy = pltpu.make_async_remote_copy(
+        src_ref=source,
+        dst_ref=target,
+        send_sem=send,
+        recv_sem=receive,
+        device_id=peer,
+        device_id_type=MESH,
+    )
+    copy.start()
+    return copy
+
+
+def halo_kernel(count, gathers, head_ref, tail_ref, *refs):
+    if gathers:
+        block_ref, above_ref, below_ref, all_ref, edge_send, edge_recv, send, recv, own = refs
+    else:
+        above_ref, below_ref, edge_send, edge_recv = refs
+    slide, me = lax.axis_index("slide"), lax.axis_index("rows")
+    peers = [(slide, lax.rem(me + k, count)) for k in range(1, count)]
+    up, down = peers[-1], peers[0]
+    greet(peers if gathers else [up, down])
+    copies = []
+    if gathers:
+        for k in range(1, count):
+            copies.append(
+                remote(block_ref, all_ref.at[me], send.at[k], recv.at[k], peers[k - 1])
+            )
+    copies.append(remote(tail_ref, above_ref, edge_send.at[0], edge_recv.at[0], down))
+    copies.append(remote(head_ref, below_ref, edge_send.at[1], edge_recv.at[1], up))
+    if gathers:
+        mine = pltpu.make_async_copy(block_ref, all_ref.at[me], own)
+        mine.start()
+        mine.wait()
+    for copy in copies:
+        copy.wait()
+
+
+def halo(cells, count, channel_id, block=None):
     channels, height, across = cells.shape
-    count = lax.axis_size(axis)
-    above = lax.ppermute(cells[:, height - 3 :], axis, [(i, i + 1) for i in range(count - 1)])
-    below = lax.ppermute(cells[:, :3], axis, [(i + 1, i) for i in range(count - 1)])
+    gathers = block is not None
+    operands = [cells[:, :3], cells[:, height - 3 :]]
+    edge = jax.ShapeDtypeStruct((channels, 3, across), cells.dtype)
+    shapes = [edge, edge]
+    scratch = [pltpu.SemaphoreType.DMA((2,)), pltpu.SemaphoreType.DMA((2,))]
+    if gathers:
+        operands.append(block)
+        shapes.append(jax.ShapeDtypeStruct((count,) + block.shape, block.dtype))
+        scratch += [
+            pltpu.SemaphoreType.DMA((count,)),
+            pltpu.SemaphoreType.DMA((count,)),
+            pltpu.SemaphoreType.DMA,
+        ]
+    above, below, *rest = pl.pallas_call(
+        functools.partial(halo_kernel, count, gathers),
+        out_shape=tuple(shapes),
+        in_specs=[VMEM] * len(operands),
+        out_specs=(VMEM,) * len(shapes),
+        scratch_shapes=scratch,
+        compiler_params=pltpu.CompilerParams(collective_id=channel_id, has_side_effects=True),
+        name="halo",
+    )(*operands)
+    me = lax.axis_index("rows")
+    above = jnp.where(me > 0, above, jnp.zeros_like(above))
+    below = jnp.where(me < count - 1, below, jnp.zeros_like(below))
     spare = jnp.zeros((channels, SLOT - height - 6, across), cells.dtype)
-    return jnp.concatenate([above, cells, below, spare], axis=1)
+    return jnp.concatenate([above, cells, below, spare], axis=1), *rest
+
+
+def sum_kernel(slides, count, part_ref, out_ref, near, half, far, send, recv):
+    slide, me = lax.axis_index("slide"), lax.axis_index("rows")
+    across = [(lax.rem(slide + k, slides), me) for k in range(1, slides)]
+    along = [(slide, lax.rem(me + k, count)) for k in range(1, count)]
+    greet(across + along)
+    first = [
+        remote(part_ref.at[peer[0]], near.at[k], send.at[0, k], recv.at[0, k], peer)
+        for k, peer in enumerate(across)
+    ]
+    for copy in first:
+        copy.wait()
+    total = part_ref[slide].astype(jnp.float32)
+    for k in range(slides - 1):
+        total = total + near[k].astype(jnp.float32)
+    half[...] = total.astype(jnp.bfloat16)
+    second = [
+        remote(half.at[peer[1]], far.at[k], send.at[1, k], recv.at[1, k], peer)
+        for k, peer in enumerate(along)
+    ]
+    for copy in second:
+        copy.wait()
+    total = half[me].astype(jnp.float32)
+    for k in range(count - 1):
+        total = total + far[k].astype(jnp.float32)
+    out_ref[slide, me] = total.astype(jnp.bfloat16)
+    third = [
+        remote(out_ref.at[slide, me], out_ref.at[slide, me], send.at[2, k], recv.at[2, k], peer)
+        for k, peer in enumerate(along)
+    ]
+    for copy in third:
+        copy.wait()
+    fourth = [
+        remote(out_ref.at[slide], out_ref.at[slide], send.at[3, k], recv.at[3, k], peer)
+        for k, peer in enumerate(across)
+    ]
+    for copy in fourth:
+        copy.wait()
+
+
+def sum_everywhere(rows, slides, count):
+    length, across = rows.shape
+    share = 16 * pl.cdiv(length, 16 * slides * count)
+    padded = jnp.pad(rows, ((0, slides * count * share - length), (0, 0))).astype(jnp.bfloat16)
+    shape = (slides, count, share, across)
+    totals = pl.pallas_call(
+        functools.partial(sum_kernel, slides, count),
+        out_shape=jax.ShapeDtypeStruct(shape, jnp.bfloat16),
+        in_specs=[VMEM],
+        out_specs=VMEM,
+        scratch_shapes=[
+            pltpu.VMEM((slides - 1,) + shape[1:], jnp.bfloat16),
+            pltpu.VMEM(shape[1:], jnp.bfloat16),
+            pltpu.VMEM((count - 1,) + shape[2:], jnp.bfloat16),
+            pltpu.SemaphoreType.DMA((4, max(slides, count) - 1)),
+            pltpu.SemaphoreType.DMA((4, max(slides, count) - 1)),
+        ],
+        compiler_params=pltpu.CompilerParams(collective_id=2, has_side_effects=True),
+        name="sum_everywhere",
+    )(padded.reshape(shape))
+    return totals.reshape(-1, across)[:length].astype(jnp.float32)
 
 
 def shifted_stack(rows):
@@ -213,7 +344,9 @@
     rows_hi = lax.reduce_precision(rows, 8, 7)
     rows_lo = rows - rows_hi
     rows_back = tap_rows(taps[:, ::-1, ::-1])
-    gathered = lax.all_gather(tile_cotangent, "rows", axis=1, tiled=True)[0]
+    slides, count = lax.axis_size("slide"), lax.axis_size("rows")
+    extended, gathered = halo(image, count, 0, tile_cotangent[0])
+    gathered = gathered.reshape(count * tiles_here, channels)
     positions = lax.dynamic_slice_in_dim(
         aggregator_order[0], lax.axis_index("rows") * tiles_here, tiles_here
     )
@@ -242,7 +375,7 @@
         compiler_params=pltpu.CompilerParams(vmem_limit_bytes=56 * 1024 * 1024),
         name="forward_block",
     )(
-        extended_rows(image, "rows"),
+        extended,
         rows_hi,
         rows_lo,
         depth_bias[:, None],
@@ -258,6 +391,7 @@
     embedding = (
         embed.reshape(channels, tiles_here, TILE).sum(axis=2) / (height * TILE)
     ).T[None]
+    (grad_extended,) = halo(grad_conv, count, 1)
     input_grad, kernel_rows = pl.pallas_call(
         backward_kernel,
         out_shape=(
@@ -268,19 +402,25 @@
         out_specs=(VMEM,) * 2,
         compiler_params=pltpu.CompilerParams(vmem_limit_bytes=40 * 1024 * 1024),
         name="backward_conv",
-    )(extended_rows(grad_conv, "rows"), image, rows_back, cotangent)
+    )(grad_extended, image, rows_back, cotangent)
     kernel_term = taps_of(kernel_rows)[:, ::-1, ::-1].reshape(channels, 49)
-    loss_norm = 1.0 / math.sqrt(lax.axis_size("slide") * lax.axis_size("rows") * height * across)
-    combined = (
-        jnp.concatenate(
-            [up_term, down_term, kernel_term, jnp.zeros((channels, 15), f32)], axis=1
-        )
-        * loss_norm
+    loss_norm = 1.0 / math.sqrt(slides * count * height * across)
+    tap_lanes = kernel_term.shape[1]
+    wide = jnp.pad(kernel_term, ((0, 0), (0, across - tap_lanes)))
+    blocks = hidden_units // across
+    combined = jnp.concatenate(
+        [
+            up_term.reshape(channels, blocks, across).transpose(1, 0, 2),
+            down_term.reshape(channels, blocks, across).transpose(1, 0, 2),
+            wide[None],
+        ],
+        axis=0,
     )
-    totals = lax.psum(combined, ("slide", "rows"))
-    grad_up = totals[:, :hidden_units]
-    grad_down = totals[:, hidden_units : 2 * hidden_units].T
-    grad_kernel = totals[:, 2 * hidden_units : 2 * hidden_units + 49]
+    totals = sum_everywhere((combined * loss_norm).reshape(-1, across), slides, count)
+    totals = totals.reshape(2 * blocks + 1, channels, across)
+    grad_up = totals[:blocks].transpose(1, 0, 2).reshape(channels, hidden_units)
+    grad_down = totals[blocks : 2 * blocks].transpose(0, 2, 1).reshape(hidden_units, channels)
+    grad_kernel = totals[2 * blocks, :, :tap_lanes]
     return (embedding, input_grad[None], grad_up, grad_down, grad_kernel)
 
 

time: 290 us -> 164 us (0.57)
  waiting for transfers between devices: 135 us -> 0 us
  Pallas kernels: 66.4 us -> 127 us
  blocking collectives: 32.9 us -> 0 us
  between operations: 14.3 us -> 0.95 us
  starting transfers between devices: 10.7 us -> 0 us
  local copies, waits for them, and re-layouts: 19.3 us -> 23.2 us
    psum x1 -> x0, waiting for transfers between devices: 130 us -> none  [on_device(): totals = lax.psum(combined, ('slide', 'rows'))]
    pallas_call x0 -> x3, Pallas kernels: none -> 61.1 us  [the longest x1 30.8 us: sum_everywhere(): pl.pallas_call(functools.partial(sum_kernel, slides, count), out_shape=ja...]
    all_gather x1 -> x0, blocking collectives: 32.9 us -> none  [on_device(): gathered = lax.all_gather(tile_cotangent, 'rows', axis=1, tiled=True)[0]]
    ppermute x4 -> x0, starting transfers between devices: 10.7 us -> none  [the longest x2 8.12 us: extended_rows(): lax.ppermute(cells[:, height - 3:], axis, [(i, i + 1) for i in range(coun...]
    ppermute x4 -> x0, waiting for transfers between devices: 4.52 us -> none  [the longest x2 4.52 us: extended_rows(): lax.ppermute(cells[:, :3], axis, [(i + 1, i) for i in range(count - 1)])]
  transfers between devices with their start and end apart: 5 -> 0, of which waited for: 2 -> 0; matrix products, arithmetic and copies ran while one was open for 5% -> 0% of each run, Pallas kernels for 0% -> 0%
where the time goes in v2:
time: 164 us; the launch traced here: 163 us
  Pallas kernels  127 us (77%)
  local copies, waits for them, and re-layouts  23.2 us (14%)
  other arithmetic  11.1 us (7%)
    pallas_call x1, Pallas kernels, on_device(): pl.pallas_call(forward_kernel, out_shape=(jax.ShapeDtypeStruct((channels,...  35 us
    pallas_call x1, Pallas kernels, on_device(): pl.pallas_call(backward_kernel, out_shape=(jax.ShapeDtypeStruct((channels...  31.4 us
    pallas_call x1, Pallas kernels, sum_everywhere(): pl.pallas_call(functools.partial(sum_kernel, slides, count), out_shape=ja...  30.8 us
    pallas_call x2, Pallas kernels, halo(): pl.pallas_call(functools.partial(halo_kernel, count, gathers), out_shape=...  30.4 us
    unnamed x40, local copies, waits for them, and re-layouts  5.76 us
    concatenate x2, other arithmetic, halo(): return (jnp.concatenate([above, cells, below, spare], axis=1), *rest)  5.12 us
    slice x2, local copies, waits for them, and re-layouts, halo(): operands = [cells[:, :3], cells[:, height - 3:]]  4.17 us

profile of v2, /device:TPU:0, one launch (start us, length us, event | category | flops | bytes accessed | tf_op | source)
XLA Modules:
  0.0 162.7 jit_solution(10986932898420865012)
XLA Ops:
  0.6 2.1 %fusion.3 = (bf16[192,3,128]{2,1,0:T(4,128)(2,1)}, bf16[192,3,128]{2,1,0:T(4,128)(2,1)}) fusion(bf16[192,32,128]{2,1,0:T(8,128)(2,1)} %bitcast.81), kind=kLoop, calls=%fused_computation.35 | loop fusion | bytes 589824 | tf_op jit(solution)/shard_map/slice | solution.py:67
  2.8 17.5 %halo.2 = (bf16[192,3,128]{2,1,0:T(4,128)(2,1)}, bf16[192,3,128]{2,1,0:T(4,128)(2,1)}, bf16[8,4,192]{2,1,0:T(4,128)(2,1)}) custom-call(bf16[192,3,128]{2,1,0:T(4,128)(2,1)} %get-tuple-element.45.head_ref, bf16[192,3,128]{2,1,0:T(4,128)(2,1)} %get-tuple-element.44.tail_ref, bf16[4,192]{1,0:T(4,128)(2,1)} %bitcast.100), custom_call_target="tpu_custom_call" | custom-call | tf_op jit(solution)/shard_map/halo/pallas_call | solution.py:79
  20.3 1.1 broadcast_select_fusion.1
  21.6 2.5 %maximum_maximum_fusion.ext_ref = bf16[192,40,128]{2,1,0:T(8,128)(2,1)} fusion(bf16[192,3,128]{2,1,0:T(4,128)(2,1)S(1)} %get-tuple-element.54, bf16[192,32,128]{2,1,0:T(8,128)(2,1)S(1)} %bitcast.82, bf16[192,3,128]{2,1,0:T(4,128)(2,1)S(1)} %get-tuple-element.55, bf16[40]{0:T(256)(128)(2,1)S(1)} %pad.39.clone), kind=kLoop, calls=%fused_computation.1 | loop fusion | flops 7864320 | bytes 3833936 | tf_op jit(solution)/shard_map/concatenate | solution.py:92
  25.2 0.8 multiply_convert_fusion
  26.1 0.6 copy-done.5
  26.8 0.9 bitcast_subtract_fusion
  27.7 0.9 broadcast_in_dim.53.up_bias
  28.6 0.9 copy.69.down_ref
  29.5 0.8 copy.65.conv_bias
  30.3 0.8 copy.66.gain_ref
  31.1 0.8 copy.67.bias_ref
  31.8 0.8 copy.70.down_bias
  32.6 35.0 %forward_block.1 = (bf16[192,32,128]{2,1,0:T(8,128)(2,1)}, f32[192,128]{1,0:T(8,128)}, f32[192,768]{1,0:T(8,128)}, f32[192,768]{1,0:T(8,128)}) custom-call(bf16[192,40,128]{2,1,0:T(8,128)(2,1)} %maximum_maximum_fusion.ext_ref, f32[3,192,128]{2,1,0:T(8,128)} %get-tuple-element.49.taps_hi, f32[3,192,128]{2,1,0:T(8,128)} %get-tuple-element.48.taps_lo, ...), custom_call_target="tpu_custom_call" | custom-call | tf_op jit(solution)/shard_map/forward_block/pallas_call | solution.py:359
  67.6 2.0 %fusion.2 = (bf16[192,3,128]{2,1,0:T(4,128)(2,1)}, bf16[192,3,128]{2,1,0:T(4,128)(2,1)}) fusion(bf16[192,32,128]{2,1,0:T(8,128)(2,1)} %get-tuple-element.20), kind=kLoop, calls=%fused_computation.34 | loop fusion | bytes 589824 | tf_op jit(solution)/shard_map/slice | solution.py:67
  69.6 12.8 %halo.3 = (bf16[192,3,128]{2,1,0:T(4,128)(2,1)}, bf16[192,3,128]{2,1,0:T(4,128)(2,1)}) custom-call(bf16[192,3,128]{2,1,0:T(4,128)(2,1)} %get-tuple-element.43.head_ref, bf16[192,3,128]{2,1,0:T(4,128)(2,1)} %get-tuple-element.42.tail_ref), custom_call_target="tpu_custom_call" | custom-call | tf_op jit(solution)/shard_map/halo/pallas_call | solution.py:79
  82.5 1.0 broadcast_select_fusion
  83.6 2.6 %maximum_maximum_fusion.1.grad_ref = bf16[192,40,128]{2,1,0:T(8,128)(2,1)S(1)} fusion(bf16[192,3,128]{2,1,0:T(4,128)(2,1)S(1)} %broadcast_select_fusion, bf16[192,32,128]{2,1,0:T(8,128)(2,1)} %get-tuple-element.20, bf16[192,3,128]{2,1,0:T(4,128)(2,1)S(1)} %broadcast_select_fusion.2, bf16[40]{0:T(256)(128)(2,1)S(1)} %pad.39.clone), kind=kLoop, calls=%fused_computation.2 | loop fusion | flops 7864320 | bytes 3833936 | tf_op jit(solution)/shard_map/concatenate | solution.py:92
  86.2 1.4 rev.6
  87.6 1.6 pad.25
  89.2 1.9 %copy.73 = f32[192,3,120]{2,0,1:T(8,128)} copy(f32[192,3,120]{0,2,1:T(8,128)} %bitcast.92) | data formatting | bytes 552960 | tf_op jit(solution)/shard_map/reshape | solution.py:313
  91.1 1.0 pad_bitcast_fusion.taps_ref
  92.0 0.9 copy-done.2
  92.9 31.4 %backward_conv.1 = (bf16[192,32,128]{2,1,0:T(8,128)(2,1)}, f32[3,192,128]{2,1,0:T(8,128)S(1)}) custom-call(bf16[192,40,128]{2,1,0:T(8,128)(2,1)S(1)} %maximum_maximum_fusion.1.grad_ref, bf16[192,32,128]{2,1,0:T(8,128)(2,1)S(1)} %bitcast.83, f32[3,192,128]{2,1,0:T(8,128)S(1)} %pad_bitcast_fusion.taps_ref, f32[192,128]{1,0:T(8,128)S(1)} %copy-done.2), custom_call_target="tpu_custom_call" | custom-call | tf_op jit(solution)/shard_map/backward_conv/pallas_call | solution.py:395
  124.8 0.6 copy-done.4
  125.8 0.9 pad.28
  126.7 30.8 %sum_everywhere.1 = bf16[4,8,80,128]{3,2,1,0:T(8,128)(2,1)} custom-call(bf16[4,8,80,128]{3,2,1,0:T(8,128)(2,1)} %bitcast.87), custom_call_target="tpu_custom_call" | custom-call | tf_op jit(solution)/shard_map/sum_everywhere/pallas_call | solution.py:139
  157.4 1.2 slice_convert_fusion
  159.1 0.9 copy.93
  160.4 0.9 copy.94
  161.3 0.7 copy.82
  162.1 0.6 multiply_bitcast_fusion
  (68 shorter events, 3.3 us)
Async XLA Ops:
  0.6 20.9 %copy-start = (bf16[1,192,32,128]{3,2,1,0:T(8,128)(2,1)S(1)}, bf16[1,192,32,128]{3,2,1,0:T(8,128)(2,1)}, u32[]{:S(2)}) copy-start(bf16[1,192,32,128]{3,2,1,0:T(8,128)(2,1)} %param.13) | copy-start | bytes 4718596
  21.5 2.5 %copy-start.16 = (s32[1,32]{1,0:T(1,128)S(1)}, s32[1,32]{1,0:T(1,128)}, u32[]{:S(2)}) copy-start(s32[1,32]{1,0:T(1,128)} %param.24) | copy-start | bytes 388
  21.5 2.6 %copy-start.9 = (bf16[8,4,192]{2,1,0:T(4,128)(2,1)S(1)}, bf16[8,4,192]{2,1,0:T(4,128)(2,1)}, u32[]{:S(2)}) copy-start(bf16[8,4,192]{2,1,0:T(4,128)(2,1)} %get-tuple-element.18) | copy-start | bytes 36868
  21.5 3.5 %copy-start.17 = (s32[1,1,4]{2,1,0:T(1,128)S(1)}, s32[1,1,4]{2,1,0:T(1,128)}, u32[]{:S(2)}) copy-start(s32[1,1,4]{2,1,0:T(1,128)} %param.23) | copy-start | bytes 52
  21.5 3.7 %copy-start.11 = (f32[192]{0:T(256)S(1)}, f32[192]{0:T(256)}, u32[]{:S(2)}) copy-start(f32[192]{0:T(256)} %param.22) | copy-start | bytes 2308
  21.5 4.4 %copy-start.8 = (f32[192,49]{0,1:T(8,128)S(1)}, f32[192,49]{0,1:T(8,128)}, u32[]{:S(2)}) copy-start(f32[192,49]{0,1:T(8,128)} %param.14) | copy-start | bytes 112900
  24.0 3.6 %copy-start.10 = (f32[768]{0:T(1024)S(1)}, f32[768]{0:T(1024)}, u32[]{:S(2)}) copy-start(f32[768]{0:T(1024)} %param.19) | copy-start | bytes 9220
  24.0 4.6 %copy-start.6 = (bf16[768,192]{0,1:T(8,128)(2,1)S(1)}, bf16[768,192]{0,1:T(8,128)(2,1)}, u32[]{:S(2)}) copy-start(bf16[768,192]{0,1:T(8,128)(2,1)} %param.20) | copy-start | bytes 884740
  24.7 4.8 %copy-start.12 = (f32[192]{0:T(256)S(1)}, f32[192]{0:T(256)}, u32[]{:S(2)}) copy-start(f32[192]{0:T(256)} %param.15) | copy-start | bytes 2308
  24.9 5.4 %copy-start.13 = (f32[192]{0:T(256)S(1)}, f32[192]{0:T(256)}, u32[]{:S(2)}) copy-start(f32[192]{0:T(256)} %param.16) | copy-start | bytes 2308
  24.9 6.1 %copy-start.14 = (f32[192]{0:T(256)S(1)}, f32[192]{0:T(256)}, u32[]{:S(2)}) copy-start(f32[192]{0:T(256)} %param.17) | copy-start | bytes 2308
  25.0 7.6 %copy-start.1 = (f32[192,128]{1,0:T(8,128)}, f32[192,128]{1,0:T(8,128)S(1)}, u32[]{:S(2)}) copy-start(f32[192,128]{1,0:T(8,128)S(1)} %copy.64.cotangent_ref) | copy-start | bytes 294916
  25.0 6.8 %copy-start.15 = (f32[192]{0:T(256)S(1)}, f32[192]{0:T(256)}, u32[]{:S(2)}) copy-start(f32[192]{0:T(256)} %param.21) | copy-start | bytes 2308
  26.0 0.6 copy-start.5
  92.0 0.9 copy-start.2
  124.3 1.1 copy-start.4
  124.3 1.2 copy-start.3
  159.1 2.9 %copy-start.7 = (f32[192,128]{1,0:T(8,128)S(1)}, f32[192,128]{1,0:T(8,128)}, u32[]{:S(2)}) copy-start(f32[192,128]{1,0:T(8,128)} %get-tuple-element.19) | copy-start | bytes 294916

commit v3 on v2

--- a/solution.py
+++ b/solution.py
@@ -64,8 +64,9 @@
 def halo(cells, count, channel_id, block=None):
     channels, height, across = cells.shape
     gathers = block is not None
-    operands = [cells[:, :3], cells[:, height - 3 :]]
-    edge = jax.ShapeDtypeStruct((channels, 3, across), cells.dtype)
+    turned = cells.transpose(1, 0, 2)
+    operands = [turned[:3], turned[height - 3 :]]
+    edge = jax.ShapeDtypeStruct((3, channels, across), cells.dtype)
     shapes = [edge, edge]
     scratch = [pltpu.SemaphoreType.DMA((2,)), pltpu.SemaphoreType.DMA((2,))]
     if gathers:
@@ -89,6 +90,7 @@
     above = jnp.where(me > 0, above, jnp.zeros_like(above))
     below = jnp.where(me < count - 1, below, jnp.zeros_like(below))
     spare = jnp.zeros((channels, SLOT - height - 6, across), cells.dtype)
+    above, below = above.transpose(1, 0, 2), below.transpose(1, 0, 2)
     return jnp.concatenate([above, cells, below, spare], axis=1), *rest
 
 
@@ -193,10 +195,10 @@
 
 
 def forward_kernel(
-    ext_ref, taps_hi, taps_lo, conv_bias, gain_ref, bias_ref, up_ref, up_bias, down_ref,
-    down_bias, mask_ref, branch_ref,
+    ext_ref, taps_hi, taps_lo, channel_ref, up_ref, up_bias, down_ref, mask_ref, branch_ref,
     grad_ref, embed_ref, up_out, down_out, held, sums, hidden_sum, slope_gain,
 ):
+    conv_bias, gain_ref, bias_ref, down_bias = [channel_ref.at[i] for i in range(4)]
     channels, _, across = ext_ref.shape
     height = grad_ref.shape[1]
     hidden_units = up_ref.shape[1]
@@ -215,7 +217,7 @@
         ) - jnp.sum(rows[height + 3 :], axis=0, keepdims=True)
         return carry
 
-    lax.fori_loop(0, channels, conv_channel, 0, unroll=4)
+    lax.fori_loop(0, channels, conv_channel, 0, unroll=8)
 
     slope_gain[...] = jnp.dot(down_ref[...], branch_ref[...], preferred_element_type=jnp.float32)
     hidden_sum[...] = jnp.zeros_like(hidden_sum)
@@ -304,7 +306,7 @@
             kernel_ref[g, pl.ds(c, 1), :] = diagonal_sums(cross[:, g * 128 : (g + 1) * 128])
         return carry
 
-    lax.fori_loop(0, channels, channel, 0, unroll=4)
+    lax.fori_loop(0, channels, channel, 0, unroll=8)
 
 
 def tap_rows(taps):
@@ -364,7 +366,7 @@
             jax.ShapeDtypeStruct((channels, hidden_units), f32),
             jax.ShapeDtypeStruct((channels, hidden_units), f32),
         ),
-        in_specs=[VMEM] * 12,
+        in_specs=[VMEM] * 9,
         out_specs=(VMEM,) * 4,
         scratch_shapes=[
             pltpu.VMEM((height * channels, across), f32),
@@ -378,13 +380,10 @@
         extended,
         rows_hi,
         rows_lo,
-        depth_bias[:, None],
-        norm_gain[:, None],
-        norm_bias[:, None],
+        jnp.stack([depth_bias, norm_gain, norm_bias, down_bias])[:, :, None],
         up_weight,
         up_bias[:, None],
         down_weight,
-        down_bias[:, None],
         scaled_mask,
         grad_branch,
     )

time: 164 us -> 144 us (0.88)
  Pallas kernels: 127 us -> 106 us
    pallas_call x1, Pallas kernels: 31.4 us -> 19.9 us  [on_device(): pl.pallas_call(backward_kernel, out_shape=(jax.ShapeDtypeStruct((channels...]
    pallas_call x2, Pallas kernels: 30.4 us -> 26 us  [halo(): pl.pallas_call(functools.partial(halo_kernel, count, gathers), out_shape=...]
    pallas_call x1, Pallas kernels: 35 us -> 30.8 us  [on_device(): pl.pallas_call(forward_kernel, out_shape=(jax.ShapeDtypeStruct((channels,...]
    transpose x0 -> x3, other arithmetic: none -> 3.36 us  [halo(): above, below = (above.transpose(1, 0, 2), below.transpose(1, 0, 2))]
    select_n x3 -> x0, other arithmetic: 2.21 us -> none  [the longest x2 2.12 us: halo(): below = jnp.where(me < count - 1, below, jnp.zeros_like(below))]
    broadcast_in_dim x4 -> x1, local copies, waits for them, and re-layouts: 3.05 us -> 0.94 us  [on_device(): jnp.stack([depth_bias, norm_gain, norm_bias, down_bias])[:, :, None]]
    pallas_call x1 -> x2, local copies, waits for them, and re-layouts: 0.09 us -> 2.11 us  [on_device(): pl.pallas_call(forward_kernel, out_shape=(jax.ShapeDtypeStruct((channels,...]
    slice x2 -> x4, local copies, waits for them, and re-layouts: 4.17 us -> 3.49 us  [halo(): operands = [turned[:3], turned[height - 3:]]]
where the time goes in v3:
time: 144 us; the launch traced here: 142 us
  Pallas kernels  106 us (74%)
  local copies, waits for them, and re-layouts  22.4 us (16%)
  other arithmetic  12.3 us (9%)
    pallas_call x1, Pallas kernels, on_device(): pl.pallas_call(forward_kernel, out_shape=(jax.ShapeDtypeStruct((channels,...  30.8 us
    pallas_call x1, Pallas kernels, sum_everywhere(): pl.pallas_call(functools.partial(sum_kernel, slides, count), out_shape=ja...  29.7 us
    pallas_call x2, Pallas kernels, halo(): pl.pallas_call(functools.partial(halo_kernel, count, gathers), out_shape=...  26 us
    pallas_call x1, Pallas kernels, on_device(): pl.pallas_call(backward_kernel, out_shape=(jax.ShapeDtypeStruct((channels...  19.9 us
    unnamed x40, local copies, waits for them, and re-layouts  5.75 us
    concatenate x2, other arithmetic, halo(): return (jnp.concatenate([above, cells, below, spare], axis=1), *rest)  5.12 us
    slice x4, local copies, waits for them, and re-layouts, halo(): operands = [turned[:3], turned[height - 3:]]  3.49 us
    transpose x3, other arithmetic, halo(): above, below = (above.transpose(1, 0, 2), below.transpose(1, 0, 2))  3.36 us

profile of v3, /device:TPU:0, one launch (start us, length us, event | category | flops | bytes accessed | tf_op | source)
XLA Modules:
  0.0 142.1 jit_solution(6661333065478683996)
XLA Ops:
  0.6 1.4 fusion.7
  2.0 0.7 copy.77.head_ref
  2.7 0.7 copy.78.tail_ref
  3.4 15.4 %halo.2 = (bf16[3,192,128]{2,1,0:T(8,128)(2,1)}, bf16[3,192,128]{2,1,0:T(8,128)(2,1)}, bf16[8,4,192]{2,1,0:T(4,128)(2,1)}) custom-call(bf16[3,192,128]{2,1,0:T(8,128)(2,1)} %copy.77.head_ref, bf16[3,192,128]{2,1,0:T(8,128)(2,1)} %copy.78.tail_ref, bf16[4,192]{1,0:T(4,128)(2,1)} %bitcast.116), custom_call_target="tpu_custom_call" | custom-call | tf_op jit(solution)/shard_map/halo/pallas_call | solution.py:80
  18.8 1.3 fusion.3
  20.2 2.5 %maximum_maximum_fusion.ext_ref = bf16[192,40,128]{2,1,0:T(8,128)(2,1)} fusion(bf16[192,3,128]{2,1,0:T(4,128)(2,1)S(1)} %get-tuple-element.54, bf16[192,32,128]{2,1,0:T(8,128)(2,1)S(1)} %bitcast.97, bf16[192,3,128]{2,1,0:T(4,128)(2,1)S(1)} %get-tuple-element.55, bf16[40]{0:T(256)(128)(2,1)S(1)} %pad.43.clone), kind=kLoop, calls=%fused_computation.1 | loop fusion | flops 7864320 | bytes 3833936 | tf_op jit(solution)/shard_map/concatenate | solution.py:94
  23.8 0.8 multiply_convert_fusion
  25.4 0.9 bitcast_subtract_fusion
  26.4 0.9 copy.84.channel_ref
  27.3 0.9 broadcast_in_dim.41.up_bias
  28.2 0.9 copy.86.down_ref
  29.2 30.8 %forward_block.1 = (bf16[192,32,128]{2,1,0:T(8,128)(2,1)}, f32[192,128]{1,0:T(8,128)}, f32[192,768]{1,0:T(8,128)}, f32[192,768]{1,0:T(8,128)}) custom-call(bf16[192,40,128]{2,1,0:T(8,128)(2,1)} %maximum_maximum_fusion.ext_ref, f32[3,192,128]{2,1,0:T(8,128)} %get-tuple-element.49.taps_hi, f32[3,192,128]{2,1,0:T(8,128)} %get-tuple-element.48.taps_lo, ...), custom_call_target="tpu_custom_call" | custom-call | tf_op jit(solution)/shard_map/forward_block/pallas_call | solution.py:361
  59.9 2.0 %copy.125 = bf16[192,32,128]{2,0,1:T(8,128)(2,1)S(1)} copy(bf16[192,32,128]{2,1,0:T(8,128)(2,1)} %get-tuple-element.20) | data formatting | bytes 3145728 | tf_op jit(solution)/shard_map/forward_block/pallas_call | solution.py:361
  61.9 0.7 fusion.6
  62.7 10.7 %halo.3 = (bf16[3,192,128]{2,1,0:T(8,128)(2,1)}, bf16[3,192,128]{2,1,0:T(8,128)(2,1)}) custom-call(bf16[3,192,128]{2,1,0:T(8,128)(2,1)} %get-tuple-element.43.head_ref, bf16[3,192,128]{2,1,0:T(8,128)(2,1)} %get-tuple-element.42.tail_ref), custom_call_target="tpu_custom_call" | custom-call | tf_op jit(solution)/shard_map/halo/pallas_call | solution.py:80
  73.3 1.1 fusion.2
  74.4 1.1 fusion.1
  75.4 2.6 %maximum_maximum_fusion.1.grad_ref = bf16[192,40,128]{2,1,0:T(8,128)(2,1)S(1)} fusion(bf16[192,3,128]{2,1,0:T(4,128)(2,1)S(1)} %fusion.1, bf16[192,32,128]{2,1,0:T(8,128)(2,1)} %get-tuple-element.20, bf16[192,3,128]{2,1,0:T(4,128)(2,1)S(1)} %fusion.2, bf16[40]{0:T(256)(128)(2,1)S(1)} %pad.43.clone), kind=kLoop, calls=%fused_computation.2 | loop fusion | flops 7864320 | bytes 3833936 | tf_op jit(solution)/shard_map/concatenate | solution.py:94
  78.1 1.4 rev.6
  79.5 1.6 %pad.25 = f32[192,9,40]{0,2,1:T(8,128)} pad(f32[192,7,7]{0,2,1:T(8,128)} %bitcast.115, f32[]{:T(128)} %constant.15.clone.1), padding=0_0x0_2x0_33 | pad | bytes 314116 | tf_op jit(solution)/shard_map/jit(_pad)/pad | solution.py:314
  81.1 1.9 %copy.92 = f32[192,3,120]{2,0,1:T(8,128)} copy(f32[192,3,120]{0,2,1:T(8,128)} %bitcast.108) | data formatting | bytes 552960 | tf_op jit(solution)/shard_map/reshape | solution.py:315
  82.9 1.0 pad_bitcast_fusion.taps_ref
  83.9 0.9 copy-done.2
  84.8 19.9 %backward_conv.1 = (bf16[192,32,128]{2,1,0:T(8,128)(2,1)}, f32[3,192,128]{2,1,0:T(8,128)S(1)}) custom-call(bf16[192,40,128]{2,1,0:T(8,128)(2,1)S(1)} %maximum_maximum_fusion.1.grad_ref, bf16[192,32,128]{2,1,0:T(8,128)(2,1)S(1)} %bitcast.98, f32[3,192,128]{2,1,0:T(8,128)S(1)} %pad_bitcast_fusion.taps_ref, f32[192,128]{1,0:T(8,128)S(1)} %copy-done.2), custom_call_target="tpu_custom_call" | custom-call | tf_op jit(solution)/shard_map/backward_conv/pallas_call | solution.py:394
  105.2 0.6 copy-done.4
  106.1 0.9 pad.28
  107.0 29.7 %sum_everywhere.1 = bf16[4,8,80,128]{3,2,1,0:T(8,128)(2,1)} custom-call(bf16[4,8,80,128]{3,2,1,0:T(8,128)(2,1)} %bitcast.102), custom_call_target="tpu_custom_call" | custom-call | tf_op jit(solution)/shard_map/sum_everywhere/pallas_call | solution.py:141
  136.8 1.2 slice_convert_fusion
  138.4 0.9 copy.126
  139.7 0.9 copy.127
  140.6 0.7 copy.101
  141.5 0.6 multiply_bitcast_fusion
  (69 shorter events, 3.8 us)
Async XLA Ops:
  0.6 19.5 %copy-start = (bf16[1,192,32,128]{3,2,1,0:T(8,128)(2,1)S(1)}, bf16[1,192,32,128]{3,2,1,0:T(8,128)(2,1)}, u32[]{:S(2)}) copy-start(bf16[1,192,32,128]{3,2,1,0:T(8,128)(2,1)} %param.13) | copy-start | bytes 4718596
  20.1 2.5 %copy-start.16 = (s32[1,32]{1,0:T(1,128)S(1)}, s32[1,32]{1,0:T(1,128)}, u32[]{:S(2)}) copy-start(s32[1,32]{1,0:T(1,128)} %param.24) | copy-start | bytes 388
  20.1 2.6 %copy-start.9 = (bf16[8,4,192]{2,1,0:T(4,128)(2,1)S(1)}, bf16[8,4,192]{2,1,0:T(4,128)(2,1)}, u32[]{:S(2)}) copy-start(bf16[8,4,192]{2,1,0:T(4,128)(2,1)} %get-tuple-element.18) | copy-start | bytes 36868
  20.1 3.5 %copy-start.17 = (s32[1,1,4]{2,1,0:T(1,128)S(1)}, s32[1,1,4]{2,1,0:T(1,128)}, u32[]{:S(2)}) copy-start(s32[1,1,4]{2,1,0:T(1,128)} %param.23) | copy-start | bytes 52
  20.1 3.7 %copy-start.11 = (f32[192]{0:T(256)S(1)}, f32[192]{0:T(256)}, u32[]{:S(2)}) copy-start(f32[192]{0:T(256)} %param.22) | copy-start | bytes 2308
  20.2 4.4 %copy-start.8 = (f32[192,49]{0,1:T(8,128)S(1)}, f32[192,49]{0,1:T(8,128)}, u32[]{:S(2)}) copy-start(f32[192,49]{0,1:T(8,128)} %param.14) | copy-start | bytes 112900
  22.6 3.7 %copy-start.12 = (f32[192]{0:T(256)S(1)}, f32[192]{0:T(256)}, u32[]{:S(2)}) copy-start(f32[192]{0:T(256)} %param.21) | copy-start | bytes 2308
  22.6 3.7 %copy-start.13 = (f32[192]{0:T(256)S(1)}, f32[192]{0:T(256)}, u32[]{:S(2)}) copy-start(f32[192]{0:T(256)} %param.17) | copy-start | bytes 2308
  22.6 3.7 %copy-start.14 = (f32[192]{0:T(256)S(1)}, f32[192]{0:T(256)}, u32[]{:S(2)}) copy-start(f32[192]{0:T(256)} %param.16) | copy-start | bytes 2308
  22.6 3.7 %copy-start.15 = (f32[192]{0:T(256)S(1)}, f32[192]{0:T(256)}, u32[]{:S(2)}) copy-start(f32[192]{0:T(256)} %param.15) | copy-start | bytes 2308
  22.7 4.6 %copy-start.10 = (f32[768]{0:T(1024)S(1)}, f32[768]{0:T(1024)}, u32[]{:S(2)}) copy-start(f32[768]{0:T(1024)} %param.19) | copy-start | bytes 9220
  22.7 5.6 %copy-start.6 = (bf16[768,192]{0,1:T(8,128)(2,1)S(1)}, bf16[768,192]{0,1:T(8,128)(2,1)}, u32[]{:S(2)}) copy-start(bf16[768,192]{0,1:T(8,128)(2,1)} %param.20) | copy-start | bytes 884740
  23.6 5.5 %copy-start.1 = (f32[192,128]{1,0:T(8,128)}, f32[192,128]{1,0:T(8,128)S(1)}, u32[]{:S(2)}) copy-start(f32[192,128]{1,0:T(8,128)S(1)} %copy.83.cotangent_ref) | copy-start | bytes 294916
  24.6 0.6 copy-start.5
  83.9 0.9 copy-start.2
  104.7 1.1 copy-start.4
  104.7 1.2 copy-start.3
  138.4 2.9 %copy-start.7 = (f32[192,128]{1,0:T(8,128)S(1)}, f32[192,128]{1,0:T(8,128)}, u32[]{:S(2)}) copy-start(f32[192,128]{1,0:T(8,128)} %get-tuple-element.19) | copy-start | bytes 294916

commit v4 on v3

--- a/solution.py
+++ b/solution.py
@@ -3,6 +3,7 @@
 
 import jax
 import jax.numpy as jnp
+import numpy as np
 from jax import lax
 from jax.experimental import pallas as pl
 from jax.experimental.pallas import tpu as pltpu
@@ -23,7 +24,7 @@
     pl.semaphore_wait(barrier, len(peers))
 
 
-def remote(source, target, send, receive, peer):
+def remote(source, target, send, receive, peer, start=True):
     copy = pltpu.make_async_remote_copy(
         src_ref=source,
         dst_ref=target,
@@ -32,7 +33,8 @@
         device_id=peer,
         device_id_type=MESH,
     )
-    copy.start()
+    if start:
+        copy.start()
     return copy
 
 
@@ -44,21 +46,26 @@
     slide, me = lax.axis_index("slide"), lax.axis_index("rows")
     peers = [(slide, lax.rem(me + k, count)) for k in range(1, count)]
     up, down = peers[-1], peers[0]
+    has_up, has_down = me > 0, me < count - 1
     greet(peers if gathers else [up, down])
-    copies = []
+    downward = remote(tail_ref, above_ref, edge_send.at[0], edge_recv.at[0], down, False)
+    upward = remote(head_ref, below_ref, edge_send.at[1], edge_recv.at[1], up, False)
+    pl.when(has_down)(downward.start)
+    pl.when(has_up)(upward.start)
     if gathers:
-        for k in range(1, count):
-            copies.append(
-                remote(block_ref, all_ref.at[me], send.at[k], recv.at[k], peers[k - 1])
-            )
-    copies.append(remote(tail_ref, above_ref, edge_send.at[0], edge_recv.at[0], down))
-    copies.append(remote(head_ref, below_ref, edge_send.at[1], edge_recv.at[1], up))
-    if gathers:
+        copies = [
+            remote(block_ref, all_ref.at[me], send.at[k], recv.at[k], peers[k - 1])
+            for k in range(1, count)
+        ]
         mine = pltpu.make_async_copy(block_ref, all_ref.at[me], own)
         mine.start()
         mine.wait()
-    for copy in copies:
-        copy.wait()
+        for copy in copies:
+            copy.wait()
+    pl.when(has_down)(downward.wait_send)
+    pl.when(has_up)(upward.wait_send)
+    pl.when(has_up)(downward.wait_recv)
+    pl.when(has_down)(upward.wait_recv)
 
 
 def halo(cells, count, channel_id, block=None):
@@ -175,10 +182,11 @@
     return jnp.concatenate(pieces, axis=0).astype(jnp.bfloat16)
 
 
-def banded(taps_ref, c, height):
+def banded(taps_ref, c, first, height):
     parts = []
     for g in range(3):
-        part = jnp.broadcast_to(taps_ref[g, pl.ds(c, 1), :], (height, 128))
+        part = taps_ref[first + g, pl.ds(c, 1), :]
+        part = jnp.broadcast_to(part, (height, 128))
         parts.append(pltpu.roll(part, 0, 1, stride=1, stride_axis=0))
     return jnp.concatenate(parts, axis=1)
 
@@ -195,7 +203,7 @@
 
 
 def forward_kernel(
-    ext_ref, taps_hi, taps_lo, channel_ref, up_ref, up_bias, down_ref, mask_ref, branch_ref,
+    ext_ref, taps_ref, channel_ref, up_ref, up_bias, down_ref, mask_ref, branch_ref,
     grad_ref, embed_ref, up_out, down_out, held, sums, hidden_sum, slope_gain,
 ):
     conv_bias, gain_ref, bias_ref, down_bias = [channel_ref.at[i] for i in range(4)]
@@ -207,8 +215,8 @@
     def conv_channel(c, carry):
         rows = ext_ref[c].astype(jnp.float32)
         stack = shifted_stack(rows)
-        hi = banded(taps_hi, c, height)
-        lo = banded(taps_lo, c, height)
+        hi = banded(taps_ref, c, 0, height)
+        lo = banded(taps_ref, channels + c, 0, height)
         left = jnp.concatenate([hi, lo], axis=0).astype(jnp.bfloat16)[:, :depth]
         both = jnp.dot(left, stack, preferred_element_type=jnp.float32)
         held[pl.ds(c, height, stride=channels), :] = both[:height] + both[height:]
@@ -292,7 +300,7 @@
 
     def channel(c, carry):
         stack = shifted_stack(grad_ref[c].astype(jnp.float32))
-        left = banded(taps_ref, c, height).astype(jnp.bfloat16)[:, :depth]
+        left = banded(taps_ref, c, 3, height).astype(jnp.bfloat16)[:, :depth]
         conv = jnp.dot(left, stack, preferred_element_type=jnp.float32)
         out_ref[c] = (conv + cotangent_ref[pl.ds(c, 1), :]).astype(jnp.bfloat16)
         spare = jnp.zeros((3 * 128 - depth, across), jnp.bfloat16)
@@ -309,11 +317,13 @@
     lax.fori_loop(0, channels, channel, 0, unroll=8)
 
 
-def tap_rows(taps):
-    channels = taps.shape[0]
-    by_column = jnp.pad(taps.transpose(0, 2, 1), ((0, 0), (0, 2), (0, SLOT - 7)))
-    groups = by_column.reshape(channels, 3, PER * SLOT)
-    return jnp.pad(groups, ((0, 0), (0, 0), (0, 128 - PER * SLOT))).transpose(1, 0, 2)
+def tap_lanes_of(mirrored):
+    places = np.zeros((49, 3 * 128), np.float32)
+    for a in range(7):
+        for b in range(7):
+            tap = 7 * (6 - a) + 6 - b if mirrored else 7 * a + b
+            places[tap, 128 * (b // PER) + SLOT * (b % PER) + a] = 1.0
+    return places
 
 
 def taps_of(rows):
@@ -341,11 +351,17 @@
     channels, height, across = image.shape
     tiles_here = across // TILE
     hidden_units = up_weight.shape[1]
-    taps = depth_kernel.reshape(channels, 7, 7)
-    rows = tap_rows(taps)
-    rows_hi = lax.reduce_precision(rows, 8, 7)
-    rows_lo = rows - rows_hi
-    rows_back = tap_rows(taps[:, ::-1, ::-1])
+    taps_hi = lax.reduce_precision(depth_kernel, 8, 7)
+    taps_lo = depth_kernel - taps_hi
+    both = jnp.concatenate([taps_hi, taps_lo], axis=0).astype(jnp.bfloat16)
+    places = np.concatenate([tap_lanes_of(False), tap_lanes_of(True)], axis=1)
+    places = places.reshape(49, 6, 128).transpose(1, 0, 2)
+    rows = lax.dot_general(
+        jnp.broadcast_to(both, (6,) + both.shape),
+        jnp.asarray(places, jnp.bfloat16),
+        (((2,), (1,)), ((0,), (0,))),
+        preferred_element_type=jnp.float32,
+    )
     slides, count = lax.axis_size("slide"), lax.axis_size("rows")
     extended, gathered = halo(image, count, 0, tile_cotangent[0])
     gathered = gathered.reshape(count * tiles_here, channels)
@@ -366,7 +382,7 @@
             jax.ShapeDtypeStruct((channels, hidden_units), f32),
             jax.ShapeDtypeStruct((channels, hidden_units), f32),
         ),
-        in_specs=[VMEM] * 9,
+        in_specs=[VMEM] * 8,
         out_specs=(VMEM,) * 4,
         scratch_shapes=[
             pltpu.VMEM((height * channels, across), f32),
@@ -378,8 +394,7 @@
         name="forward_block",
     )(
         extended,
-        rows_hi,
-        rows_lo,
+        rows,
         jnp.stack([depth_bias, norm_gain, norm_bias, down_bias])[:, :, None],
         up_weight,
         up_bias[:, None],
@@ -401,7 +416,7 @@
         out_specs=(VMEM,) * 2,
         compiler_params=pltpu.CompilerParams(vmem_limit_bytes=40 * 1024 * 1024),
         name="backward_conv",
-    )(grad_extended, image, rows_back, cotangent)
+    )(grad_extended, image, rows, cotangent)
     kernel_term = taps_of(kernel_rows)[:, ::-1, ::-1].reshape(channels, 49)
     loss_norm = 1.0 / math.sqrt(slides * count * height * across)
     tap_lanes = kernel_term.shape[1]

time: 144 us -> 144 us (level)
  local copies, waits for them, and re-layouts: 22.4 us -> 19.5 us
    reshape x4 -> x0, local copies, waits for them, and re-layouts: 2.05 us -> none  [the longest x2 2.02 us: tap_rows(): groups = by_column.reshape(channels, 3, PER * SLOT)]
    transpose x1, local copies, waits for them, and re-layouts: 0.04 us -> 1.92 us  [on_device(): up_term.reshape(channels, blocks, across).transpose(1, 0, 2)]
    transpose x1, local copies, waits for them, and re-layouts: 0.04 us -> 1.92 us  [on_device(): down_term.reshape(channels, blocks, across).transpose(1, 0, 2)]
    pad x2 -> x0, local copies, waits for them, and re-layouts: 1.61 us -> none  [tap_rows(): jnp.pad(taps.transpose(0, 2, 1), ((0, 0), (0, 2), (0, SLOT - 7)))]
    concatenate x2, other arithmetic: 5.12 us -> 3.64 us  [halo(): return (jnp.concatenate([above, cells, below, spare], axis=1), *rest)]
    unnamed x40 -> x18, local copies, waits for them, and re-layouts: 5.75 us -> 5.37 us
where the time goes in v4:
time: 144 us; the launch traced here: 142 us
  Pallas kernels  107 us (74%)
  local copies, waits for them, and re-layouts  19.5 us (14%)
  other arithmetic  13.7 us (10%)
    pallas_call x1, Pallas kernels, on_device(): pl.pallas_call(forward_kernel, out_shape=(jax.ShapeDtypeStruct((channels,...  30.9 us
    pallas_call x1, Pallas kernels, sum_everywhere(): pl.pallas_call(functools.partial(sum_kernel, slides, count), out_shape=ja...  30.8 us
    pallas_call x2, Pallas kernels, halo(): pl.pallas_call(functools.partial(halo_kernel, count, gathers), out_shape=...  25 us
    pallas_call x1, Pallas kernels, on_device(): pl.pallas_call(backward_kernel, out_shape=(jax.ShapeDtypeStruct((channels...  19.9 us
    unnamed x18, local copies, waits for them, and re-layouts  5.37 us
    concatenate x2, other arithmetic, halo(): return (jnp.concatenate([above, cells, below, spare], axis=1), *rest)  3.64 us
    transpose x3, other arithmetic, halo(): above, below = (above.transpose(1, 0, 2), below.transpose(1, 0, 2))  3.36 us

profile of v4, /device:TPU:0, one launch (start us, length us, event | category | flops | bytes accessed | tf_op | source)
XLA Modules:
  0.0 142.0 jit_solution(16634080024123513208)
XLA Ops:
  0.7 0.8 convert_bitcast_fusion.1
  1.4 0.7 fusion.8
  2.2 0.7 compare_and_fusion
  3.1 0.7 maximum_bitcast_fusion
  3.9 0.8 reduce-precision_convert_fusion
  4.8 1.0 copy.75.channel_ref
  5.7 1.6 %broadcast_in_dim.45.up_bias = f32[768,1]{1,0:T(8,128)} reshape(f32[768]{0:T(1024)} %param.20) | data formatting | bytes 6144 | tf_op jit(solution)/shard_map/broadcast_in_dim | solution.py:400
  7.4 1.9 %copy.77.down_ref = bf16[768,192]{1,0:T(8,128)(2,1)} copy(bf16[768,192]{0,1:T(8,128)(2,1)} %param.21) | data formatting | bytes 589824 | tf_op args[7]
  9.5 0.7 copy.71.tail_ref
  10.1 0.7 copy.70.head_ref
  10.8 14.4 %halo.2 = (bf16[3,192,128]{2,1,0:T(8,128)(2,1)}, bf16[3,192,128]{2,1,0:T(8,128)(2,1)}, bf16[8,4,192]{2,1,0:T(4,128)(2,1)}) custom-call(bf16[3,192,128]{2,1,0:T(8,128)(2,1)} %copy.70.head_ref, bf16[3,192,128]{2,1,0:T(8,128)(2,1)} %copy.71.tail_ref, bf16[4,192]{1,0:T(4,128)(2,1)} %bitcast.99), custom_call_target="tpu_custom_call" | custom-call | tf_op jit(solution)/shard_map/halo/pallas_call | solution.py:87
  25.2 0.7 reshape.91
  26.6 1.3 fusion.3
  28.0 0.7 multiply_convert_fusion
  28.7 1.4 fusion.5.taps_ref
  30.1 2.5 %maximum_maximum_fusion.ext_ref = bf16[192,40,128]{2,1,0:T(8,128)(2,1)} fusion(bf16[192,3,128]{2,1,0:T(4,128)(2,1)S(1)} %get-tuple-element.52, bf16[192,32,128]{2,1,0:T(8,128)(2,1)S(1)} %bitcast.84, bf16[192,3,128]{2,1,0:T(4,128)(2,1)S(1)} %get-tuple-element.53, bf16[40]{0:T(256)(128)(2,1)S(1)} %pad.27.clone), kind=kLoop, calls=%fused_computation.1 | loop fusion | flops 7864320 | bytes 3833936 | tf_op jit(solution)/shard_map/concatenate | solution.py:101
  32.6 30.9 %forward_block.1 = (bf16[192,32,128]{2,1,0:T(8,128)(2,1)}, f32[192,128]{1,0:T(8,128)}, f32[192,768]{1,0:T(8,128)}, f32[192,768]{1,0:T(8,128)}) custom-call(bf16[192,40,128]{2,1,0:T(8,128)(2,1)} %maximum_maximum_fusion.ext_ref, f32[6,384,128]{2,1,0:T(8,128)} %fusion.5.taps_ref, f32[4,192,1]{2,1,0:T(8,128)} %copy.75.channel_ref, bf16[192,768]{1,0:T(8,128)(2,1)} %up_ref.1, ...), custom_call_target="tpu_custom_call" | custom-call | tf_op jit(solution)/shard_map/forward_block/pallas_call | solution.py:377
  63.5 1.1 copy.78
  65.3 1.9 %bitcast_bitcast_fusion.1 = f32[6,192,128]{2,1,0:T(8,128)} fusion(f32[192,768]{1,0:T(8,128)} %get-tuple-element.24), kind=kLoop, calls=%fused_computation.10 | loop fusion | bytes 1179648 | tf_op jit(solution)/shard_map/transpose | solution.py:427
  67.2 1.9 %bitcast_bitcast_fusion = f32[6,192,128]{2,1,0:T(8,128)} fusion(f32[192,768]{1,0:T(8,128)} %get-tuple-element.25), kind=kLoop, calls=%fused_computation.9 | loop fusion | bytes 1179648 | tf_op jit(solution)/shard_map/transpose | solution.py:428
  69.7 0.7 fusion.9
  70.5 10.7 %halo.3 = (bf16[3,192,128]{2,1,0:T(8,128)(2,1)}, bf16[3,192,128]{2,1,0:T(8,128)(2,1)}) custom-call(bf16[3,192,128]{2,1,0:T(8,128)(2,1)} %get-tuple-element.43.head_ref, bf16[3,192,128]{2,1,0:T(8,128)(2,1)} %get-tuple-element.42.tail_ref), custom_call_target="tpu_custom_call" | custom-call | tf_op jit(solution)/shard_map/halo/pallas_call | solution.py:87
  81.1 1.1 fusion.2
  82.2 1.1 fusion.1
  83.2 1.2 maximum_maximum_fusion.1.grad_ref
  84.5 19.9 %backward_conv.1 = (bf16[192,32,128]{2,1,0:T(8,128)(2,1)}, f32[3,192,128]{2,1,0:T(8,128)S(1)}) custom-call(bf16[192,40,128]{2,1,0:T(8,128)(2,1)S(1)} %maximum_maximum_fusion.1.grad_ref, bf16[192,32,128]{2,1,0:T(8,128)(2,1)S(1)} %bitcast.85, f32[6,384,128]{2,1,0:T(8,128)S(1)} %copy-done, f32[192,128]{1,0:T(8,128)S(1)} %copy.74.cotangent_ref), custom_call_target="tpu_custom_call" | custom-call | tf_op jit(solution)/shard_map/backward_conv/pallas_call | solution.py:409
  105.8 0.9 pad.10
  106.7 30.8 %sum_everywhere.1 = bf16[4,8,80,128]{3,2,1,0:T(8,128)(2,1)} custom-call(bf16[4,8,80,128]{3,2,1,0:T(8,128)(2,1)} %bitcast.89), custom_call_target="tpu_custom_call" | custom-call | tf_op jit(solution)/shard_map/sum_everywhere/pallas_call | solution.py:148
  137.5 1.2 slice_convert_fusion
  138.6 0.7 copy.90
  139.8 0.9 copy.114
  141.1 0.9 copy.113
  (41 shorter events, 4.7 us)
Async XLA Ops:
  0.6 8.7 %copy-start.1 = (bf16[1,192,32,128]{3,2,1,0:T(8,128)(2,1)S(1)}, bf16[1,192,32,128]{3,2,1,0:T(8,128)(2,1)}, u32[]{:S(2)}) copy-start(bf16[1,192,32,128]{3,2,1,0:T(8,128)(2,1)} %param.14) | copy-start | bytes 4718596
  5.7 22.2 %copy-start.6 = (f32[192]{0:T(256)S(1)}, f32[192]{0:T(256)}, u32[]{:S(2)}) copy-start(f32[192]{0:T(256)} %param.23) | copy-start | bytes 2308
  7.4 21.4 %copy-start.5 = (bf16[6,49,128]{2,1,0:T(8,128)(2,1)S(1)}, bf16[6,49,128]{2,1,0:T(8,128)(2,1)}, u32[]{:S(2)}) copy-start(bf16[6,49,128]{2,1,0:T(8,128)(2,1)} %constant.41.clone) | copy-start | bytes 225796
  63.5 5.6 %copy-start.2 = (bf16[192,32,128]{2,1,0:T(8,128)(2,1)S(1)}, bf16[192,32,128]{2,1,0:T(8,128)(2,1)}, u32[]{:S(2)}) copy-start(bf16[192,32,128]{2,1,0:T(8,128)(2,1)} %get-tuple-element.20) | copy-start | bytes 4718596
  83.2 1.3 copy-start
  104.4 1.1 copy-start.3
  104.4 1.2 copy-start.4
